TPU v7x, 32 devices: a whole 2x2x4 slice. The times are simulated.
32 devices in a mesh: dp: 4 (over y, x), fsdp: 8 (over z, core).
Axes of the slice: x: 2, y: 2, z: 4, core: 2. Of those that a mesh axis runs over, the one named last changes fastest.
Arguments:
- tokens: bfloat16 [4096, 768], P(('dp', 'fsdp')), may hold values from -6 to 6
- cotangent: bfloat16 [4096, 768], P(('dp', 'fsdp')), may hold values from -6 to 6
- segments: int32 [32, 128], P(('dp', 'fsdp')), may hold values from 0 to 7, never falling along the last dimension, each value on 1 to 64 neighbouring positions
- w_qkv: float32 [768, 2304], P(('dp', 'fsdp')), may hold values from -0.21875 to 0.21875
- w_out: float32 [768, 768], P(('dp', 'fsdp')), may hold values from -0.4375 to 0.4375
- w_up: float32 [768, 3072], P(('dp', 'fsdp')), may hold values from -0.21875 to 0.21875
- w_down: float32 [3072, 768], P(('dp', 'fsdp')), may hold values from -0.109375 to 0.109375
- vectors: float32 [9984], P(('dp', 'fsdp')), may hold values from -0.9 to 1.5
- first_qkv: float32 [768, 2304], P(('dp', 'fsdp')), may hold values from -1 to 1
- first_out: float32 [768, 768], P(('dp', 'fsdp')), may hold values from -1 to 1
- first_up: float32 [768, 3072], P(('dp', 'fsdp')), may hold values from -1 to 1
- first_down: float32 [3072, 768], P(('dp', 'fsdp')), may hold values from -1 to 1
- first_vec: float32 [9984], P(('dp', 'fsdp')), may hold values from -1 to 1
- second_qkv: float32 [768, 2304], P(('dp', 'fsdp')), may hold values from 0.02 to 0.2
- second_out: float32 [768, 768], P(('dp', 'fsdp')), may hold values from 0.02 to 0.2
- second_up: float32 [768, 3072], P(('dp', 'fsdp')), may hold values from 0.02 to 0.2
- second_down: float32 [3072, 768], P(('dp', 'fsdp')), may hold values from 0.02 to 0.2
- second_vec: float32 [9984], P(('dp', 'fsdp')), may hold values from 0.02 to 0.2
Outputs:
- output: bfloat16 [4096, 768], P(('dp', 'fsdp'))
- grad_tokens: bfloat16 [4096, 768], P(('dp', 'fsdp'))
- grad_w_qkv: float32 [768, 2304], P(('dp', 'fsdp'))
- grad_w_out: float32 [768, 768], P(('dp', 'fsdp'))
- grad_w_up: float32 [768, 3072], P(('dp', 'fsdp'))
- grad_w_down: float32 [3072, 768], P(('dp', 'fsdp'))
- grad_vectors: float32 [9984], P(('dp', 'fsdp'))
- new_w_qkv: float32 [768, 2304], P(('dp', 'fsdp'))
- new_w_out: float32 [768, 768], P(('dp', 'fsdp'))
- new_w_up: float32 [768, 3072], P(('dp', 'fsdp'))
- new_w_down: float32 [3072, 768], P(('dp', 'fsdp'))
- new_vectors: float32 [9984], P(('dp', 'fsdp'))
- new_first_qkv: float32 [768, 2304], P(('dp', 'fsdp'))
- new_first_out: float32 [768, 768], P(('dp', 'fsdp'))
- new_first_up: float32 [768, 3072], P(('dp', 'fsdp'))
- new_first_down: float32 [3072, 768], P(('dp', 'fsdp'))
- new_first_vec: float32 [9984], P(('dp', 'fsdp'))
- new_second_qkv: float32 [768, 2304], P(('dp', 'fsdp'))
- new_second_out: float32 [768, 768], P(('dp', 'fsdp'))
- new_second_up: float32 [768, 3072], P(('dp', 'fsdp'))
- new_second_down: float32 [3072, 768], P(('dp', 'fsdp'))
- new_second_vec: float32 [9984], P(('dp', 'fsdp'))
Inputs may be any that keep to these rules, and one draw needn't show every extreme that they name: `segments`: in each row the numbers never fall; every number 0 to 7 names 1 to 64 consecutive tokens, and one names exactly 64.
All inputs are finite; a program needn't handle non-finite values.
Results may differ from a plain program's by a relative error of at most 0.012.
Values may be sent and summed in bfloat16 or wider, within the bound.
A program may use at most 128 MiB of HBM per device.

v0:
```python
import math

import jax
import jax.numpy as jnp
from jax import lax
from jax.sharding import PartitionSpec as P

D = 768
HEADS = 12
HEAD_DIM = 64
ROT = 16
STEP = 3


eps_norm = 1e-05
beta_first = 0.9
beta_second = 0.95
adam_epsilon = 1e-08
rate_matrix = 0.008
rate_vector = 0.1
decay_matrix = 0.01
rotary_base = 10000.0
mask_fill = -1e30


def layer_norm(inputs, gain_row, offset):
    center = inputs - jnp.mean(inputs, axis=-1, keepdims=True)
    inv_sigma = lax.rsqrt(jnp.mean(center * center, axis=-1, keepdims=True) + eps_norm)
    normed = center * inv_sigma
    return (normed, inv_sigma, normed * gain_row + offset)


def layer_norm_back(grad_norm, normed, inv_sigma, gain_row):
    scaled = grad_norm * gain_row
    return inv_sigma * (
        scaled
        - jnp.mean(scaled, axis=-1, keepdims=True)
        - normed * jnp.mean(scaled * normed, axis=-1, keepdims=True)
    )


def gelu_value(inputs):
    return 0.5 * inputs * (1.0 + jax.scipy.special.erf(inputs * (1.0 / math.sqrt(2.0))))


def gelu_slope(inputs):
    cumulative = 0.5 * (1.0 + jax.scipy.special.erf(inputs * (1.0 / math.sqrt(2.0))))
    return cumulative + inputs * jnp.exp(-0.5 * inputs * inputs) * (1.0 / math.sqrt(2.0 * math.pi))


def rotary_tables(segment):
    rows_here = segment.shape[0]
    earlier = jnp.sum((segment[None, :] < segment[:, None]).astype(jnp.int32), axis=1)
    position = jnp.arange(rows_here, dtype=jnp.int32) - earlier
    half_rot = ROT // 2
    inverse = rotary_base ** (-2.0 * jnp.arange(half_rot, dtype=jnp.float32) / ROT)
    angles = position.astype(jnp.float32)[:, None] * inverse[None, :]
    return (jnp.cos(angles)[:, None, :], jnp.sin(angles)[:, None, :])


def rotate(tensor, cosine_part, sine_part):
    half_rot = ROT // 2
    front_part = tensor[..., :half_rot]
    middle = tensor[..., half_rot:ROT]
    remain = tensor[..., ROT:]
    return jnp.concatenate(
        [
            front_part * cosine_part - middle * sine_part,
            middle * cosine_part + front_part * sine_part,
            remain,
        ],
        axis=-1,
    )


def rotate_back(tensor, cosine_part, sine_part):
    half_rot = ROT // 2
    front_part = tensor[..., :half_rot]
    middle = tensor[..., half_rot:ROT]
    remain = tensor[..., ROT:]
    return jnp.concatenate(
        [
            front_part * cosine_part + middle * sine_part,
            middle * cosine_part - front_part * sine_part,
            remain,
        ],
        axis=-1,
    )


def doc_mask(segment):
    row_index = jnp.arange(segment.shape[0], dtype=jnp.int32)
    return (segment[:, None] == segment[None, :]) & (row_index[None, :] <= row_index[:, None])


def masked_scores(queries, key_rot, allowed):
    scores = jnp.einsum("qhd,khd->hqk", queries, key_rot, preferred_element_type=jnp.float32) * (
        1.0 / math.sqrt(HEAD_DIM)
    )
    return jnp.where(allowed[None, :, :], scores, mask_fill)


def forward_pass(
    tokens, allowed, cosine_part, sine_part, full_qkv, full_out, full_up, full_down, full_vec
):
    rows_here = tokens.shape[0]
    vec_table = full_vec.astype(jnp.float32).reshape(13, D)
    inputs = tokens.astype(jnp.float32)
    normed_one, sigma_one, hidden_one = layer_norm(inputs, vec_table[0], vec_table[1])
    normed_two, sigma_two, hidden_two = layer_norm(inputs, vec_table[2], vec_table[3])
    hidden_one = hidden_one.astype(jnp.bfloat16)
    hidden_two = hidden_two.astype(jnp.bfloat16)
    projected = jnp.dot(hidden_one, full_qkv, preferred_element_type=jnp.float32) + vec_table[
        4:7
    ].reshape(-1)
    queries = rotate(
        projected[:, :D].reshape(rows_here, HEADS, HEAD_DIM), cosine_part, sine_part
    ).astype(jnp.bfloat16)
    key_rot = rotate(
        projected[:, D : 2 * D].reshape(rows_here, HEADS, HEAD_DIM), cosine_part, sine_part
    ).astype(jnp.bfloat16)
    values = projected[:, 2 * D :].reshape(rows_here, HEADS, HEAD_DIM).astype(jnp.bfloat16)
    scores = masked_scores(queries, key_rot, allowed)
    top_score = jnp.max(scores, axis=-1, keepdims=True)
    log_total = top_score + jnp.log(jnp.sum(jnp.exp(scores - top_score), axis=-1, keepdims=True))
    soft_weights = jnp.exp(scores - log_total).astype(jnp.bfloat16)
    context = (
        jnp.einsum("hqk,khd->qhd", soft_weights, values, preferred_element_type=jnp.float32)
        .reshape(rows_here, D)
        .astype(jnp.bfloat16)
    )
    attended = jnp.dot(context, full_out, preferred_element_type=jnp.float32) + vec_table[7]
    up_proj = jnp.dot(hidden_two, full_up, preferred_element_type=jnp.float32) + vec_table[
        8:12
    ].reshape(-1)
    activated = gelu_value(up_proj).astype(jnp.bfloat16)
    feed_out = jnp.dot(activated, full_down, preferred_element_type=jnp.float32) + vec_table[12]
    output = (inputs + attended + feed_out).astype(jnp.bfloat16)
    saved = (
        normed_one,
        sigma_one,
        hidden_one,
        normed_two,
        sigma_two,
        hidden_two,
        queries,
        key_rot,
        values,
        log_total,
        context,
        up_proj,
        activated,
    )
    return (output, saved)


def backward_pass(
    saved,
    cotangent,
    allowed,
    cosine_part,
    sine_part,
    back_qkv,
    back_out,
    back_up,
    back_down,
    back_vec,
):
    (
        normed_one,
        sigma_one,
        hidden_one,
        normed_two,
        sigma_two,
        hidden_two,
        queries,
        key_rot,
        values,
        log_total,
        context,
        up_proj,
        activated,
    ) = saved
    rows_here = cotangent.shape[0]
    vec_table = back_vec.astype(jnp.float32).reshape(13, D)
    grad_out = cotangent.astype(jnp.float32)
    grad_w_down = jnp.dot(activated.T, cotangent, preferred_element_type=jnp.float32)
    grad_act = jnp.dot(cotangent, back_down.T, preferred_element_type=jnp.float32)
    grad_up = grad_act * gelu_slope(up_proj)
    grad_up_low = grad_up.astype(jnp.bfloat16)
    grad_w_up = jnp.dot(hidden_two.T, grad_up_low, preferred_element_type=jnp.float32)
    grad_hidden_two = jnp.dot(grad_up_low, back_up.T, preferred_element_type=jnp.float32)
    grad_w_out = jnp.dot(context.T, cotangent, preferred_element_type=jnp.float32)
    grad_context = (
        jnp.dot(cotangent, back_out.T, preferred_element_type=jnp.float32)
        .astype(jnp.bfloat16)
        .reshape(rows_here, HEADS, HEAD_DIM)
    )
    again_scores = masked_scores(queries, key_rot, allowed)
    probs_full = jnp.exp(again_scores - log_total)
    probs_low = probs_full.astype(jnp.bfloat16)
    grad_probs = jnp.einsum(
        "qhd,khd->hqk", grad_context, values, preferred_element_type=jnp.float32
    )
    row_inner = jnp.sum(probs_full * grad_probs, axis=-1, keepdims=True)
    grad_scores = (probs_full * (grad_probs - row_inner) * (1.0 / math.sqrt(HEAD_DIM))).astype(
        jnp.bfloat16
    )
    grad_queries = jnp.einsum(
        "hqk,khd->qhd", grad_scores, key_rot, preferred_element_type=jnp.float32
    )
    grad_keys = jnp.einsum("hqk,qhd->khd", grad_scores, queries, preferred_element_type=jnp.float32)
    grad_values = jnp.einsum(
        "hqk,qhd->khd", probs_low, grad_context, preferred_element_type=jnp.float32
    )
    grad_projected = jnp.concatenate(
        [
            rotate_back(grad_queries, cosine_part, sine_part).reshape(rows_here, D),
            rotate_back(grad_keys, cosine_part, sine_part).reshape(rows_here, D),
            grad_values.reshape(rows_here, D),
        ],
        axis=1,
    )
    grad_proj_low = grad_projected.astype(jnp.bfloat16)
    grad_w_qkv = jnp.dot(hidden_one.T, grad_proj_low, preferred_element_type=jnp.float32)
    grad_hidden_one = jnp.dot(grad_proj_low, back_qkv.T, preferred_element_type=jnp.float32)
    grad_table = jnp.concatenate(
        [
            jnp.sum(grad_hidden_one * normed_one, axis=0)[None],
            jnp.sum(grad_hidden_one, axis=0)[None],
            jnp.sum(grad_hidden_two * normed_two, axis=0)[None],
            jnp.sum(grad_hidden_two, axis=0)[None],
            jnp.sum(grad_projected, axis=0).reshape(3, D),
            jnp.sum(grad_out, axis=0)[None],
            jnp.sum(grad_up, axis=0).reshape(4, D),
            jnp.sum(grad_out, axis=0)[None],
        ],
        axis=0,
    )
    grad_tokens = (
        grad_out
        + layer_norm_back(grad_hidden_one, normed_one, sigma_one, vec_table[0])
        + layer_norm_back(grad_hidden_two, normed_two, sigma_two, vec_table[2])
    ).astype(jnp.bfloat16)
    return (grad_tokens, grad_w_qkv, grad_w_out, grad_w_up, grad_w_down, grad_table.reshape(-1))


def adam_update(weight, gradient, moment_one, moment_two, rate_value, decay_value):
    new_one = beta_first * moment_one + (1.0 - beta_first) * gradient
    new_two = beta_second * moment_two + (1.0 - beta_second) * gradient * gradient
    corrected_one = new_one / (1.0 - beta_first**STEP)
    corrected_two = new_two / (1.0 - beta_second**STEP)
    new_weight = weight - rate_value * (
        corrected_one / (jnp.sqrt(corrected_two) + adam_epsilon) + decay_value * weight
    )
    return (new_weight, new_one, new_two)


def per_device(
    tokens,
    cotangent,
    segments,
    w_qkv,
    w_out,
    w_up,
    w_down,
    vectors,
    first_qkv,
    first_out,
    first_up,
    first_down,
    first_vec,
    second_qkv,
    second_out,
    second_up,
    second_down,
    second_vec,
):
    device_count = lax.axis_size(("dp", "fsdp"))
    segment = segments[0]
    allowed = doc_mask(segment)
    cosine_part, sine_part = rotary_tables(segment)
    low_qkv = w_qkv.astype(jnp.bfloat16)
    low_out = w_out.astype(jnp.bfloat16)
    low_vec = vectors.astype(jnp.bfloat16)
    low_up = w_up.astype(jnp.bfloat16)
    low_down = w_down.astype(jnp.bfloat16)
    full_qkv, full_out, full_vec, full_up, full_down = (
        lax.all_gather(low_qkv, ("dp", "fsdp"), axis=0, tiled=True),
        lax.all_gather(low_out, ("dp", "fsdp"), axis=0, tiled=True),
        lax.all_gather(low_vec, ("dp", "fsdp"), axis=0, tiled=True),
        lax.all_gather(low_up, ("dp", "fsdp"), axis=0, tiled=True),
        lax.all_gather(low_down, ("dp", "fsdp"), axis=0, tiled=True),
    )
    output, saved = forward_pass(
        tokens, allowed, cosine_part, sine_part, full_qkv, full_out, full_up, full_down, full_vec
    )
    back_qkv, back_out, back_vec, back_up, back_down = (
        lax.all_gather(low_qkv, ("dp", "fsdp"), axis=0, tiled=True),
        lax.all_gather(low_out, ("dp", "fsdp"), axis=0, tiled=True),
        lax.all_gather(low_vec, ("dp", "fsdp"), axis=0, tiled=True),
        lax.all_gather(low_up, ("dp", "fsdp"), axis=0, tiled=True),
        lax.all_gather(low_down, ("dp", "fsdp"), axis=0, tiled=True),
    )
    grad_tokens, local_qkv, local_out, local_up, local_down, local_vec = backward_pass(
        saved,
        cotangent,
        allowed,
        cosine_part,
        sine_part,
        back_qkv,
        back_out,
        back_up,
        back_down,
        back_vec,
    )
    factor = 1.0 / math.sqrt(device_count * tokens.shape[0])
    summed_qkv, summed_out, summed_vec, summed_up, summed_down = (
        lax.psum_scatter(local_qkv, ("dp", "fsdp"), scatter_dimension=0, tiled=True),
        lax.psum_scatter(local_out, ("dp", "fsdp"), scatter_dimension=0, tiled=True),
        lax.psum_scatter(local_vec, ("dp", "fsdp"), scatter_dimension=0, tiled=True),
        lax.psum_scatter(local_up, ("dp", "fsdp"), scatter_dimension=0, tiled=True),
        lax.psum_scatter(local_down, ("dp", "fsdp"), scatter_dimension=0, tiled=True),
    )
    grad_w_qkv = summed_qkv * factor
    grad_w_out = summed_out * factor
    grad_vectors = summed_vec * factor
    grad_w_up = summed_up * factor
    grad_w_down = summed_down * factor
    new_w_qkv, new_first_qkv, new_second_qkv = adam_update(
        w_qkv, grad_w_qkv, first_qkv, second_qkv, rate_matrix, decay_matrix
    )
    new_w_out, new_first_out, new_second_out = adam_update(
        w_out, grad_w_out, first_out, second_out, rate_matrix, decay_matrix
    )
    new_w_up, new_first_up, new_second_up = adam_update(
        w_up, grad_w_up, first_up, second_up, rate_matrix, decay_matrix
    )
    new_w_down, new_first_down, new_second_down = adam_update(
        w_down, grad_w_down, first_down, second_down, rate_matrix, decay_matrix
    )
    new_vectors, new_first_vec, new_second_vec = adam_update(
        vectors, grad_vectors, first_vec, second_vec, rate_vector, 0.0
    )
    return (
        output,
        grad_tokens,
        grad_w_qkv,
        grad_w_out,
        grad_w_up,
        grad_w_down,
        grad_vectors,
        new_w_qkv,
        new_w_out,
        new_w_up,
        new_w_down,
        new_vectors,
        new_first_qkv,
        new_first_out,
        new_first_up,
        new_first_down,
        new_first_vec,
        new_second_qkv,
        new_second_out,
        new_second_up,
        new_second_down,
        new_second_vec,
    )


def solution(mesh):
    placed = (
        P(("dp", "fsdp"), None),
        P(("dp", "fsdp"), None),
        P(("dp", "fsdp"), None),
        P(("dp", "fsdp"), None),
        P(("dp", "fsdp"), None),
        P(("dp", "fsdp"), None),
        P(("dp", "fsdp"), None),
        P(("dp", "fsdp")),
        P(("dp", "fsdp"), None),
        P(("dp", "fsdp"), None),
        P(("dp", "fsdp"), None),
        P(("dp", "fsdp"), None),
        P(("dp", "fsdp")),
        P(("dp", "fsdp"), None),
        P(("dp", "fsdp"), None),
        P(("dp", "fsdp"), None),
        P(("dp", "fsdp"), None),
        P(("dp", "fsdp")),
    )
    return jax.shard_map(
        per_device,
        mesh=mesh,
        in_specs=placed,
        out_specs=(
            P(("dp", "fsdp"), None),
            P(("dp", "fsdp"), None),
            P(("dp", "fsdp"), None),
            P(("dp", "fsdp"), None),
            P(("dp", "fsdp"), None),
            P(("dp", "fsdp"), None),
            P(("dp", "fsdp")),
            P(("dp", "fsdp"), None),
            P(("dp", "fsdp"), None),
            P(("dp", "fsdp"), None),
            P(("dp", "fsdp"), None),
            P(("dp", "fsdp")),
            P(("dp", "fsdp"), None),
            P(("dp", "fsdp"), None),
            P(("dp", "fsdp"), None),
            P(("dp", "fsdp"), None),
            P(("dp", "fsdp")),
            P(("dp", "fsdp"), None),
            P(("dp", "fsdp"), None),
            P(("dp", "fsdp"), None),
            P(("dp", "fsdp"), None),
            P(("dp", "fsdp")),
        ),
        check_vma=False,
    )
```

profile of v0, /device:TPU:9, one launch (start us, length us, event | category | flops | bytes accessed | tf_op | source)
XLA Modules:
  0.0 777.1 jit_solution(10844883370704652472)
XLA Ops:
  11.6 40.4 %all-reduce = bf16[9984]{0:T(1024)(128)(2,1)S(1)} all-reduce(bf16[9984]{0:T(1024)(128)(2,1)S(1)} %dynamic-update-slice), channel_id=1, replica_groups=mesh['dp'=4,'fsdp'=8] {'dp','fsdp'}, use_global_device_ids=true, to_apply=%add | all-reduce | flops 9984 | bytes 39936
  56.6 16.1 %all-gather.5.cloned.1.call-done = bf16[768,2304]{1,0:T(8,128)(2,1)} async-done(((bf16[24,2304]{1,0:T(8,128)(2,1)}), bf16[768,2304]{1,0:T(8,128)(2,1)}) %all-gather.5.cloned.1.call-update) | async-done | bytes 3538960 | tf_op jit(solution)/shard_map/all_gather | solution.py:289
  72.6 2.7 convolution_add_fusion
  77.1 1.9 fusion.80
  79.2 60.1 %all-gather.9.cloned.1.call-done = bf16[768,3072]{1,0:T(8,128)(2,1)} async-done(((bf16[24,3072]{1,0:T(8,128)(2,1)}), bf16[768,3072]{1,0:T(8,128)(2,1)}) %all-gather.9.cloned.1.call-update) | async-done | bytes 4718608 | tf_op jit(solution)/shard_map/all_gather | solution.py:292
  139.3 3.2 convolution_add_fusion.1
  142.5 5.1 fusion.74
  147.7 92.7 %reduce-scatter.7.cloned.1.call-done = f32[24,768]{1,0:T(8,128)} async-done(((f32[768,768]{1,0:T(8,128)}), f32[24,768]{1,0:T(8,128)}) %reduce-scatter.7.cloned.1.call-update) | async-done | bytes 73744 | tf_op jit(solution)/shard_map/reduce_scatter | solution.py:320
  242.2 138.9 %reduce-scatter.11.cloned.1.call-done = f32[96,768]{1,0:T(8,128)} async-done(((f32[3072,768]{1,0:T(8,128)}), f32[96,768]{1,0:T(8,128)}) %reduce-scatter.11.cloned.1.call-update) | async-done | bytes 294928 | tf_op jit(solution)/shard_map/reduce_scatter | solution.py:323
  381.1 2.3 multiply_subtract_fusion
  383.4 55.7 %all-gather.7.cloned.1.call-done = bf16[768,768]{1,0:T(8,128)(2,1)} async-done(((bf16[24,768]{1,0:T(8,128)(2,1)}), bf16[768,768]{1,0:T(8,128)(2,1)}) %all-gather.7.cloned.1.call-update) | async-done | bytes 1179664 | tf_op jit(solution)/shard_map/all_gather | solution.py:290
  442.3 2.0 convolution_bitcast_fusion.1
  445.1 2.5 convolution_bitcast_fusion
  451.8 4.1 fusion.66
  456.1 49.9 %all-gather.11.cloned.1.call-done = bf16[3072,768]{1,0:T(8,128)(2,1)} async-done(((bf16[96,768]{1,0:T(8,128)(2,1)}), bf16[3072,768]{1,0:T(8,128)(2,1)}) %all-gather.11.cloned.1.call-update) | async-done | bytes 4718608 | tf_op jit(solution)/shard_map/all_gather | solution.py:293
  506.0 4.7 fusion.78
  511.5 5.2 fusion.45
  518.7 108.5 %reduce-scatter.5.cloned.1.call-done = f32[24,2304]{1,0:T(8,128)} async-done(((f32[768,2304]{1,0:T(8,128)}), f32[24,2304]{1,0:T(8,128)}) %reduce-scatter.5.cloned.1.call-update) | async-done | bytes 221200 | tf_op jit(solution)/shard_map/reduce_scatter | solution.py:319
  627.2 2.2 multiply_subtract_fusion.2
  629.5 4.2 fusion.47
  637.8 40.2 %all-reduce.1 = f32[9984]{0:T(1024)S(1)} all-reduce(f32[9984]{0:T(1024)S(1)} %reshape.243), channel_id=6, replica_groups=mesh['dp'=4,'fsdp'=8] {'dp','fsdp'}, use_global_device_ids=true, to_apply=%region_21.22.clone | all-reduce | flops 9984 | bytes 79872
  678.8 3.3 convolution_add_fusion.3
  683.2 84.9 %reduce-scatter.9.cloned.1.call-done = f32[24,3072]{1,0:T(8,128)} async-done(((f32[768,3072]{1,0:T(8,128)}), f32[24,3072]{1,0:T(8,128)}) %reduce-scatter.9.cloned.1.call-update) | async-done | bytes 294928 | tf_op jit(solution)/shard_map/reduce_scatter | solution.py:322
  768.2 2.1 multiply_subtract_fusion.1
  (162 shorter events, 29.4 us)
Async XLA Ops:
  7.2 65.5 %copy-start = (bf16[128,768]{1,0:T(8,128)(2,1)S(1)}, bf16[128,768]{1,0:T(8,128)(2,1)}, u32[]{:S(2)}) copy-start(bf16[128,768]{1,0:T(8,128)(2,1)} %param.18) | copy-start | bytes 589828
  7.2 65.4 %all-gather.5.cloned.1.call-start = ((), (), s32[]{:S(2)}) async-start(), calls=%async_computation.4 | async-start | bytes 3649536 | tf_op jit(solution)/shard_map/all_gather | solution.py:289
  8.9 130.4 %all-gather.9.cloned.1.call-start = ((), (), s32[]{:S(2)}) async-start(), calls=%async_computation.6 | async-start | bytes 4866048 | tf_op jit(solution)/shard_map/all_gather | solution.py:292
  10.6 229.7 %reduce-scatter.7.cloned.1.call-start = ((), (), s32[]{:S(2)}) async-start(), calls=%async_computation.9 | async-start | bytes 2433024 | tf_op jit(solution)/shard_map/reduce_scatter | solution.py:320
  53.8 85.4 %copy-start.28 = (f32[128]{0:T(128)}, f32[128]{0:T(128)S(1)}, u32[]{:S(2)}) copy-start(f32[128]{0:T(128)S(1)} %broadcast_multiply_fusion.8) | copy-start | bytes 1540
  55.0 84.3 %copy-start.31 = (f32[128]{0:T(128)}, f32[128]{0:T(128)S(1)}, u32[]{:S(2)}) copy-start(f32[128]{0:T(128)S(1)} %add_rsqrt_fusion) | copy-start | bytes 1540
  55.1 20.9 %copy-start.26 = (f32[128,8]{0,1:T(8,128)}, f32[128,8]{0,1:T(8,128)S(1)}, u32[]{:S(2)}) copy-start(f32[128,8]{0,1:T(8,128)S(1)} %get-tuple-element.79) | copy-start | bytes 12292
  79.1 302.0 %reduce-scatter.11.cloned.1.call-start = ((), (), s32[]{:S(2)}) async-start(), calls=%async_computation.11 | async-start | bytes 9732096 | tf_op jit(solution)/shard_map/reduce_scatter | solution.py:323
  147.6 233.5 %copy-start.14 = (f32[96,768]{1,0:T(8,128)S(1)}, f32[96,768]{1,0:T(8,128)}, u32[]{:S(2)}) copy-start(f32[96,768]{1,0:T(8,128)} %param.24) | copy-start | bytes 884740
  147.6 233.5 %copy-start.15 = (f32[96,768]{1,0:T(8,128)S(1)}, f32[96,768]{1,0:T(8,128)}, u32[]{:S(2)}) copy-start(f32[96,768]{1,0:T(8,128)} %param.29) | copy-start | bytes 884740
  147.6 291.5 %all-gather.7.cloned.1.call-start = ((), (), s32[]{:S(2)}) async-start(), calls=%async_computation.5 | async-start | bytes 1216512 | tf_op jit(solution)/shard_map/all_gather | solution.py:290
  242.1 263.9 %all-gather.11.cloned.1.call-start = ((), (), s32[]{:S(2)}) async-start(), calls=%async_computation.7 | async-start | bytes 4866048 | tf_op jit(solution)/shard_map/all_gather | solution.py:293
  383.4 243.8 %reduce-scatter.5.cloned.1.call-start = ((), (), s32[]{:S(2)}) async-start(), calls=%async_computation.8 | async-start | bytes 7299072 | tf_op jit(solution)/shard_map/reduce_scatter | solution.py:319
  455.9 55.6 %copy-start.30 = (f32[128]{0:T(128)S(1)}, f32[128]{0:T(128)}, u32[]{:S(2)}) copy-start(f32[128]{0:T(128)} %copy-done.28) | copy-start | bytes 1540
  455.9 55.6 %copy-start.33 = (f32[128]{0:T(128)S(1)}, f32[128]{0:T(128)}, u32[]{:S(2)}) copy-start(f32[128]{0:T(128)} %copy-done.31) | copy-start | bytes 1540
  455.9 312.3 %reduce-scatter.9.cloned.1.call-start = ((), (), s32[]{:S(2)}) async-start(), calls=%async_computation.10 | async-start | bytes 9732096 | tf_op jit(solution)/shard_map/reduce_scatter | solution.py:322
  516.7 110.5 %copy-start.13 = (f32[24,2304]{1,0:T(8,128)S(1)}, f32[24,2304]{1,0:T(8,128)}, u32[]{:S(2)}) copy-start(f32[24,2304]{1,0:T(8,128)} %param.21) | copy-start | bytes 663556
  635.2 42.8 %copy-start.42 = (f32[312]{0:T(512)S(1)}, f32[312]{0:T(512)}, u32[]{:S(2)}) copy-start(f32[312]{0:T(512)} %param.25) | copy-start | bytes 3748
  635.2 42.8 %copy-start.43 = (f32[312]{0:T(512)S(1)}, f32[312]{0:T(512)}, u32[]{:S(2)}) copy-start(f32[312]{0:T(512)} %param.30) | copy-start | bytes 3748
  635.2 42.8 %copy-start.44 = (f32[312]{0:T(512)S(1)}, f32[312]{0:T(512)}, u32[]{:S(2)}) copy-start(f32[312]{0:T(512)} %param.35) | copy-start | bytes 3748
  635.2 43.5 %copy-start.41 = (f32[768]{0:T(1024)S(1)}, f32[768]{0:T(1024)}, u32[]{:S(2)}) copy-start(f32[768]{0:T(1024)} %get-tuple-element.73) | copy-start | bytes 9220
  682.1 86.1 %copy-start.12 = (f32[24,3072]{1,0:T(8,128)S(1)}, f32[24,3072]{1,0:T(8,128)}, u32[]{:S(2)}) copy-start(f32[24,3072]{1,0:T(8,128)} %param.23) | copy-start | bytes 884740
  682.1 86.1 %copy-start.16 = (f32[24,3072]{1,0:T(8,128)S(1)}, f32[24,3072]{1,0:T(8,128)}, u32[]{:S(2)}) copy-start(f32[24,3072]{1,0:T(8,128)} %param.28) | copy-start | bytes 884740
  682.1 86.0 %copy-start.17 = (f32[24,3072]{1,0:T(8,128)S(1)}, f32[24,3072]{1,0:T(8,128)}, u32[]{:S(2)}) copy-start(f32[24,3072]{1,0:T(8,128)} %param.33) | copy-start | bytes 884740
  (29 other events, 86.2 us)
Sparse Core Ops, SparseCore 0:
  11.6 60.9 all-gather.4
  76.2 63.0 all-gather.8
  144.6 95.6 reduce-scatter.6
  246.1 134.9 reduce-scatter.10
  384.5 54.5 all-gather.6
  442.6 63.3 all-gather.10
  511.7 115.4 reduce-scatter.4
  633.1 135.0 reduce-scatter.8
where the time goes:
time: 782 us; the launch traced here: 777 us
  waiting for transfers between devices  607 us (78%)
  blocking collectives  80.6 us (10%)
  matrix products  45.4 us (6%)
  other arithmetic  20.4 us (3%)
  between operations  14.9 us (2%)
  local copies, waits for them, and re-layouts  8.48 us (1%)
    reduce_scatter x1, waiting for transfers between devices, per_device(): lax.psum_scatter(local_down, ('dp', 'fsdp'), scatter_dimension=0, tiled=T...  139 us
    reduce_scatter x1, waiting for transfers between devices, per_device(): lax.psum_scatter(local_qkv, ('dp', 'fsdp'), scatter_dimension=0, tiled=True)  108 us
    reduce_scatter x1, waiting for transfers between devices, per_device(): lax.psum_scatter(local_out, ('dp', 'fsdp'), scatter_dimension=0, tiled=True)  92.7 us
    reduce_scatter x1, waiting for transfers between devices, per_device(): lax.psum_scatter(local_up, ('dp', 'fsdp'), scatter_dimension=0, tiled=True)  84.9 us
    unnamed x2, blocking collectives  80.6 us
    all_gather x1, waiting for transfers between devices, per_device(): lax.all_gather(low_up, ('dp', 'fsdp'), axis=0, tiled=True)  60.1 us
    all_gather x1, waiting for transfers between devices, per_device(): lax.all_gather(low_out, ('dp', 'fsdp'), axis=0, tiled=True)  55.7 us
    all_gather x1, waiting for transfers between devices, per_device(): lax.all_gather(low_down, ('dp', 'fsdp'), axis=0, tiled=True)  49.9 us
  transfers between devices with their start and end apart: 8, of which 8 were waited for; matrix products, arithmetic and copies ran while one was open for 9% of the time, Pallas kernels for 0%

commit v1 on v0

--- a/solution.py
+++ b/solution.py
@@ -1,8 +1,11 @@
+import functools
 import math
 
 import jax
 import jax.numpy as jnp
 from jax import lax
+from jax.experimental import pallas as pl
+from jax.experimental.pallas import tpu as pltpu
 from jax.sharding import PartitionSpec as P
 
 D = 768
@@ -256,6 +259,308 @@
     return (new_weight, new_one, new_two)
 
 
+MESH = pl.DeviceIdType.MESH
+LANES = 128
+VEC_WIDE = 3 * LANES
+STEP_WIDE = 5 * LANES
+
+
+class Place:
+    def __init__(self, side, fsdp):
+        self.side, self.fsdp, self.depth = side, fsdp, fsdp // 2
+        index, column = lax.axis_index("dp"), lax.axis_index("fsdp")
+        self.core, self.level = lax.rem(column, 2), lax.div(column, 2)
+        self.high, self.low = lax.div(index, side), lax.rem(index, side)
+
+    def device(self, first, second, level, owner=None, target=None):
+        owner = self.core if owner is None else owner
+        target = owner if target is None else target
+        one = lax.rem(self.low * (1 - owner) + self.high * owner + first, self.side)
+        two = lax.rem(self.high * (1 - owner) + self.low * owner + second, self.side)
+        high = two * (1 - owner) + one * owner
+        low = one * (1 - owner) + two * owner
+        return (high * self.side + low, lax.rem(self.level + level, self.depth) * 2 + target)
+
+    def rank(self, first, second, level, owner=None):
+        row, column = self.device(first, second, level, owner)
+        return row * self.fsdp + column
+
+    def greet(self):
+        barrier = pltpu.get_barrier_semaphore()
+        peers = [self.device(0, 0, 0, None, 1 - self.core)]
+        peers += [self.device(k, 0, 0) for k in range(1, self.side)]
+        peers += [self.device(0, k, 0) for k in range(1, self.side)]
+        peers += [self.device(0, 0, k) for k in range(1, self.depth)]
+        for peer in peers:
+            pl.semaphore_signal(barrier, inc=1, device_id=peer, device_id_type=MESH)
+        pl.semaphore_wait(barrier, len(peers))
+
+    def number(self, first, second, level):
+        return (second * self.side + first) * self.depth + level
+
+
+def gather_kernel(side, fsdp, *refs):
+    kinds = 2
+    shards, wholes = refs[:kinds], refs[kinds : 2 * kinds]
+    wired, paired, sent, kept = refs[2 * kinds :]
+    here = Place(side, fsdp)
+    depth = here.depth
+    half = side * side * depth
+    own = here.rank(0, 0, 0)
+    local = [
+        pltpu.make_async_copy(shards[i], wholes[i].at[own], kept.at[i]) for i in range(kinds)
+    ]
+    here.greet()
+
+    def push(origin, hop):
+        first, second, level = origin
+        slot = here.rank(first, second, level)
+        for i in range(kinds):
+            source = shards[i] if origin == (0, 0, 0) else wholes[i].at[slot]
+            if hop is None:
+                peer = here.device(0, 0, 0, None, 1 - here.core)
+                arrival = paired.at[here.number(first, second, level), i]
+            else:
+                peer = here.device(*hop)
+                arrival = wired.at[
+                    here.number(
+                        (first - hop[0]) % side, (second - hop[1]) % side, (level - hop[2]) % depth
+                    ),
+                    i,
+                ]
+            pltpu.make_async_remote_copy(
+                src_ref=source,
+                dst_ref=wholes[i].at[slot],
+                send_sem=sent.at[i],
+                recv_sem=arrival,
+                device_id=peer,
+                device_id_type=MESH,
+            ).start()
+
+    def arrive(origin, sems, owner):
+        slot = here.rank(*origin, owner)
+        for i in range(kinds):
+            pltpu.make_async_copy(
+                wholes[i].at[slot], wholes[i].at[slot], sems.at[here.number(*origin), i]
+            ).wait()
+
+    first_hops = [(k, 0, 0) for k in range(1, side)]
+    second_hops = [(0, k, 0) for k in range(1, side)]
+    level_hops = [(0, 0, k) for k in range(1, depth)]
+    for hop in second_hops + first_hops + level_hops + [None]:
+        push((0, 0, 0), hop)
+    for copy in local:
+        copy.start()
+    for level in range(1, depth):
+        arrive((0, 0, level), wired, here.core)
+        for hop in second_hops + first_hops + [None]:
+            push((0, 0, level), hop)
+    for level in range(depth):
+        for first in range(1, side):
+            arrive((first, 0, level), wired, here.core)
+            for hop in second_hops + [None]:
+                push((first, 0, level), hop)
+    for first in range(side):
+        for level in range(depth):
+            for second in range(1, side):
+                arrive((first, second, level), wired, here.core)
+                push((first, second, level), None)
+    for second in range(side):
+        for first in range(side):
+            for level in range(depth):
+                arrive((first, second, level), paired, 1 - here.core)
+    for copy in local:
+        copy.wait()
+    for i in range(kinds):
+        every = wholes[i].at[pl.ds(0, 2 * half - 1)]
+        pltpu.make_async_copy(every, every, sent.at[i]).wait()
+
+
+def gather_shards(shards, side, fsdp):
+    count = side * side * fsdp
+    half = count // 2
+    return pl.pallas_call(
+        functools.partial(gather_kernel, side, fsdp),
+        out_shape=[jax.ShapeDtypeStruct((count, *x.shape), x.dtype) for x in shards],
+        in_specs=[pl.BlockSpec(memory_space=pltpu.VMEM)] * len(shards),
+        out_specs=[pl.BlockSpec(memory_space=pl.ANY)] * len(shards),
+        scratch_shapes=[
+            pltpu.SemaphoreType.DMA((half, len(shards))),
+            pltpu.SemaphoreType.DMA((half, len(shards))),
+            pltpu.SemaphoreType.DMA((len(shards),)),
+            pltpu.SemaphoreType.DMA((len(shards),)),
+        ],
+        compiler_params=pltpu.CompilerParams(collective_id=0, has_side_effects=True),
+    )(*shards)
+
+
+def scatter_kernel(side, fsdp, *refs):
+    parts, (total,) = refs[:5], refs[5:6]
+    mine, pair, one, two, three = refs[6:11]
+    load_sem, pair_sem, wire_sem, sent_pair, sent = refs[11:]
+    here = Place(side, fsdp)
+    depth, rows = here.depth, total.shape[0]
+    wide = total.shape[1]
+    here.greet()
+
+    pieces, at = [], 0
+    for part in parts:
+        for block in range(part.shape[1] // rows):
+            pieces.append((part, block * rows, at, part.shape[2]))
+            at += part.shape[2]
+
+    firsts = list(range(1, side)) + [0]
+    levels = list(range(1, depth)) + [0]
+    order = [(f, s, k) for s in firsts for f in firsts for k in levels]
+    for first, second, level in order:
+        index = here.number(first, second, level)
+        theirs = here.rank(first, second, level, 1 - here.core)
+        ours = here.rank(first, second, level)
+        for part, row, column, width in pieces:
+            pltpu.make_async_remote_copy(
+                src_ref=part.at[theirs, pl.ds(row, rows)],
+                dst_ref=pair.at[index, :, pl.ds(column, width)],
+                send_sem=sent_pair,
+                recv_sem=pair_sem.at[index],
+                device_id=here.device(0, 0, 0, None, 1 - here.core),
+                device_id_type=MESH,
+            ).start()
+        for part, row, column, width in pieces:
+            pltpu.make_async_copy(
+                part.at[ours, pl.ds(row, rows)],
+                mine.at[index, :, pl.ds(column, width)],
+                load_sem.at[index],
+            ).start()
+
+    def send(index, target, slot, number, hop):
+        pltpu.make_async_remote_copy(
+            src_ref=mine.at[index],
+            dst_ref=target.at[slot],
+            send_sem=sent.at[index],
+            recv_sem=wire_sem.at[number],
+            device_id=here.device(*hop),
+            device_id_type=MESH,
+        ).start()
+
+    def landed(block, sem):
+        pltpu.make_async_copy(block, block, sem).wait()
+
+    second_slot = lambda second, first, level: ((second - 1) * side + first) * depth + level
+    first_slot = lambda first, level: (first - 1) * depth + level
+    base_two = (side - 1) * side * depth
+    base_three = base_two + (side - 1) * depth
+    for first, second, level in order:
+        index = here.number(first, second, level)
+        landed(mine.at[index], load_sem.at[index])
+        landed(pair.at[index], pair_sem.at[index])
+        terms = [mine.at[index], pair.at[index]]
+        if second == 0:
+            for k in range(1, side):
+                slot = second_slot(k, first, level)
+                landed(one.at[slot], wire_sem.at[slot])
+                terms.append(one.at[slot])
+            if first == 0:
+                for k in range(1, side):
+                    slot = first_slot(k, level)
+                    landed(two.at[slot], wire_sem.at[base_two + slot])
+                    terms.append(two.at[slot])
+                if level == 0:
+                    for k in range(1, depth):
+                        landed(three.at[k - 1], wire_sem.at[base_three + k - 1])
+                        terms.append(three.at[k - 1])
+        last = (first, second, level) == (0, 0, 0)
+
+        @pl.loop(0, wide // STEP_WIDE)
+        def _(step):
+            columns = pl.ds(pl.multiple_of(step * STEP_WIDE, LANES), STEP_WIDE)
+            value = terms[0][:, columns].astype(jnp.float32)
+            for term in terms[1:]:
+                value = value + term[:, columns].astype(jnp.float32)
+            if last:
+                total[:, columns] = value
+            else:
+                mine[index, :, columns] = value.astype(jnp.bfloat16)
+
+        if second:
+            slot = second_slot(second, first, level)
+            send(index, one, slot, slot, (0, second, 0))
+        elif first:
+            slot = first_slot(first, level)
+            send(index, two, slot, base_two + slot, (first, 0, 0))
+        elif level:
+            send(index, three, level - 1, base_three + level - 1, (0, 0, level))
+    landed(pair, sent_pair)
+    for first, second, level in order[:-1]:
+        index = here.number(first, second, level)
+        landed(mine.at[index], sent.at[index])
+
+
+def scatter_sums(parts, side, fsdp):
+    depth = fsdp // 2
+    half, rows = side * side * depth, parts[0].shape[1]
+    wide = sum(x.shape[1] * x.shape[2] for x in parts) // rows
+    stages = [(side - 1) * side * depth, (side - 1) * depth, depth - 1]
+    return pl.pallas_call(
+        functools.partial(scatter_kernel, side, fsdp),
+        out_shape=jax.ShapeDtypeStruct((rows, wide), jnp.float32),
+        in_specs=[pl.BlockSpec(memory_space=pl.ANY)] * 5,
+        out_specs=pl.BlockSpec(memory_space=pltpu.VMEM),
+        scratch_shapes=[
+            pltpu.VMEM((n, rows, wide), jnp.bfloat16) for n in [half, half, *stages]
+        ]
+        + [
+            pltpu.SemaphoreType.DMA((half,)),
+            pltpu.SemaphoreType.DMA((half,)),
+            pltpu.SemaphoreType.DMA((sum(stages),)),
+            pltpu.SemaphoreType.DMA,
+            pltpu.SemaphoreType.DMA((half,)),
+        ],
+        compiler_params=pltpu.CompilerParams(
+            collective_id=1, has_side_effects=True, vmem_limit_bytes=56 << 20
+        ),
+    )(*parts)
+
+
+def gather_all(w_qkv, w_out, w_up, w_down, vectors, side, fsdp):
+    rows, count = w_qkv.shape[0], side * side * fsdp
+    low = [x.astype(jnp.bfloat16) for x in (w_qkv, w_out, w_up, w_down, vectors)]
+    vec = jnp.pad(low[4], (0, rows * LANES - vectors.shape[0])).reshape(rows, LANES)
+    packed, full_down = gather_shards(
+        (jnp.concatenate([low[0], low[1], low[2], vec], axis=1), low[3]), side, fsdp
+    )
+    packed = packed.reshape(count * rows, -1)
+    ends = [w_qkv.shape[1], w_out.shape[1], w_up.shape[1]]
+    one, two, three = ends[0], ends[0] + ends[1], sum(ends)
+    full_vec = packed[:, three:].reshape(count, rows * LANES)[:, : vectors.shape[0]].reshape(-1)
+    return (
+        packed[:, :one],
+        packed[:, one:two],
+        packed[:, two:three],
+        full_down.reshape(-1, w_down.shape[1]),
+        full_vec,
+    )
+
+
+def scatter_all(local_qkv, local_out, local_up, local_down, local_vec, side, fsdp):
+    count = side * side * fsdp
+    rows, down_rows = local_qkv.shape[0] // count, local_down.shape[0] // count
+    vec_size = local_vec.shape[0] // count
+    vec = jnp.pad(
+        local_vec.reshape(count, vec_size), ((0, 0), (0, rows * LANES - vec_size))
+    ).reshape(count, rows, LANES)
+    vec = jnp.pad(vec, ((0, 0), (0, 0), (0, VEC_WIDE - LANES)))
+    parts = [x.reshape(count, x.shape[0] // count, x.shape[1]) for x in (local_qkv, local_out, local_up)]
+    parts += [vec, local_down.reshape(count, down_rows, -1)]
+    total = scatter_sums([x.astype(jnp.bfloat16) for x in parts], side, fsdp)
+    outs, at = [], 0
+    for part in parts:
+        width = part.shape[1] * part.shape[2] // rows
+        outs.append(total[:, at : at + width])
+        at += width
+    down = outs[4].reshape(rows, down_rows // rows, -1).swapaxes(0, 1).reshape(down_rows, -1)
+    return outs[0], outs[1], outs[2], down, outs[3][:, :LANES].reshape(-1)[:vec_size]
+
+
 def per_device(
     tokens,
     cotangent,
@@ -280,27 +585,27 @@
     segment = segments[0]
     allowed = doc_mask(segment)
     cosine_part, sine_part = rotary_tables(segment)
-    low_qkv = w_qkv.astype(jnp.bfloat16)
-    low_out = w_out.astype(jnp.bfloat16)
-    low_vec = vectors.astype(jnp.bfloat16)
-    low_up = w_up.astype(jnp.bfloat16)
-    low_down = w_down.astype(jnp.bfloat16)
-    full_qkv, full_out, full_vec, full_up, full_down = (
-        lax.all_gather(low_qkv, ("dp", "fsdp"), axis=0, tiled=True),
-        lax.all_gather(low_out, ("dp", "fsdp"), axis=0, tiled=True),
-        lax.all_gather(low_vec, ("dp", "fsdp"), axis=0, tiled=True),
-        lax.all_gather(low_up, ("dp", "fsdp"), axis=0, tiled=True),
-        lax.all_gather(low_down, ("dp", "fsdp"), axis=0, tiled=True),
-    )
+    axes = ("dp", "fsdp")
+    fsdp = lax.axis_size("fsdp")
+    side = math.isqrt(lax.axis_size("dp"))
+    direct = (
+        side * side == lax.axis_size("dp")
+        and fsdp % 2 == 0
+        and w_qkv.shape[0] % 8 == 0
+        and w_down.shape[0] % w_qkv.shape[0] == 0
+        and vectors.shape[0] <= w_qkv.shape[0] * LANES
+    )
+    if direct:
+        full_qkv, full_out, full_up, full_down, full_vec = gather_all(
+            w_qkv, w_out, w_up, w_down, vectors, side, fsdp
+        )
+    else:
+        full_qkv, full_out, full_up, full_down, full_vec = (
+            lax.all_gather(x.astype(jnp.bfloat16), axes, axis=0, tiled=True)
+            for x in (w_qkv, w_out, w_up, w_down, vectors)
+        )
     output, saved = forward_pass(
         tokens, allowed, cosine_part, sine_part, full_qkv, full_out, full_up, full_down, full_vec
-    )
-    back_qkv, back_out, back_vec, back_up, back_down = (
-        lax.all_gather(low_qkv, ("dp", "fsdp"), axis=0, tiled=True),
-        lax.all_gather(low_out, ("dp", "fsdp"), axis=0, tiled=True),
-        lax.all_gather(low_vec, ("dp", "fsdp"), axis=0, tiled=True),
-        lax.all_gather(low_up, ("dp", "fsdp"), axis=0, tiled=True),
-        lax.all_gather(low_down, ("dp", "fsdp"), axis=0, tiled=True),
     )
     grad_tokens, local_qkv, local_out, local_up, local_down, local_vec = backward_pass(
         saved,
@@ -308,20 +613,20 @@
         allowed,
         cosine_part,
         sine_part,
-        back_qkv,
-        back_out,
-        back_up,
-        back_down,
-        back_vec,
+        full_qkv,
+        full_out,
+        full_up,
+        full_down,
+        full_vec,
     )
     factor = 1.0 / math.sqrt(device_count * tokens.shape[0])
-    summed_qkv, summed_out, summed_vec, summed_up, summed_down = (
-        lax.psum_scatter(local_qkv, ("dp", "fsdp"), scatter_dimension=0, tiled=True),
-        lax.psum_scatter(local_out, ("dp", "fsdp"), scatter_dimension=0, tiled=True),
-        lax.psum_scatter(local_vec, ("dp", "fsdp"), scatter_dimension=0, tiled=True),
-        lax.psum_scatter(local_up, ("dp", "fsdp"), scatter_dimension=0, tiled=True),
-        lax.psum_scatter(local_down, ("dp", "fsdp"), scatter_dimension=0, tiled=True),
-    )
+    local = (local_qkv, local_out, local_up, local_down, local_vec)
+    if direct:
+        summed_qkv, summed_out, summed_up, summed_down, summed_vec = scatter_all(*local, side, fsdp)
+    else:
+        summed_qkv, summed_out, summed_up, summed_down, summed_vec = (
+            lax.psum_scatter(x, axes, scatter_dimension=0, tiled=True) for x in local
+        )
     grad_w_qkv = summed_qkv * factor
     grad_w_out = summed_out * factor
     grad_vectors = summed_vec * factor

time: 782 us -> 262 us (0.34)
  waiting for transfers between devices: 607 us -> 0 us
  Pallas kernels: 0 us -> 189 us
  blocking collectives: 80.6 us -> 0 us
  between operations: 14.9 us -> 1.5 us
    reduce_scatter x4 -> x0, waiting for transfers between devices: 425 us -> none  [the longest x1 139 us: per_device(): lax.psum_scatter(local_down, ('dp', 'fsdp'), scatter_dimension=0, tiled=T...]
    pallas_call x0 -> x2, Pallas kernels: none -> 189 us  [the longest x1 95.9 us: gather_shards(): pl.pallas_call(functools.partial(gather_kernel, side, fsdp), out_shape=[j...]
    all_gather x4 -> x0, waiting for transfers between devices: 182 us -> none  [the longest x1 60.1 us: per_device(): lax.all_gather(low_up, ('dp', 'fsdp'), axis=0, tiled=True)]
    unnamed x2 -> x0, blocking collectives: 80.6 us -> none
  transfers between devices with their start and end apart: 8 -> 0, of which waited for: 8 -> 0; matrix products, arithmetic and copies ran while one was open for 9% -> 0% of each run, Pallas kernels for 0% -> 0%
where the time goes in v1:
time: 262 us; the launch traced here: 261 us
  Pallas kernels  189 us (72%)
  matrix products  43.7 us (17%)
  other arithmetic  15.7 us (6%)
  local copies, waits for them, and re-layouts  11.4 us (4%)
    pallas_call x1, Pallas kernels, gather_shards(): pl.pallas_call(functools.partial(gather_kernel, side, fsdp), out_shape=[j...  95.9 us
    pallas_call x1, Pallas kernels, scatter_sums(): pl.pallas_call(functools.partial(scatter_kernel, side, fsdp), out_shape=j...  93.1 us

profile of v1, /device:TPU:9, one launch (start us, length us, event | category | flops | bytes accessed | tf_op | source)
XLA Modules:
  0.0 261.4 jit_solution(2061276652460246440)
XLA Ops:
  5.7 95.9 %shard_map.345 = (bf16[32,24,6272]{2,1,0:T(8,128)(2,1)}, bf16[32,96,768]{2,1,0:T(8,128)(2,1)}) custom-call(bf16[24,6272]{1,0:T(8,128)(2,1)} %pad_maximum_fusion.3.refs_0_, bf16[96,768]{1,0:T(8,128)(2,1)} %convert_element_type.117.refs_1_), custom_call_target="tpu_custom_call" | custom-call | tf_op jit(solution)/shard_map/pallas_call | solution.py:382
  103.8 3.3 %fusion.6 = f32[128,3072]{1,0:T(8,128)S(1)} fusion(bf16[768,6272]{1,0:T(8,128)(2,1)} %bitcast.98, f32[3072]{0:T(1024)S(1)} %slice.171, bf16[128,768]{1,0:T(8,128)(2,1)S(1)} %copy-done, f32[768]{0:T(1024)S(1)} %get-tuple-element.76, f32[768]{0:T(1024)S(1)} %get-tuple-element.77, f32[128]{0:T(128)S(1)} %add_rsqrt_fusion, f32[128]{0:T(128)S(1)} %broadcast_multiply_fusion.4), kind=kOutput, calls=%fused_computation.11 | convolution fusion | flops 604962816 | bytes 6507520 | tf_op jit(solution)/shard_map/dot_general | solution.py:136
  108.5 2.7 %convolution_add_fusion = f32[128,2304]{1,0:T(8,128)S(1)} fusion(bf16[768,6272]{1,0:T(8,128)(2,1)} %bitcast.99, f32[2304]{0:T(1024)S(1)} %slice.156, bf16[128,768]{1,0:T(8,128)(2,1)S(1)} %copy-done, f32[768]{0:T(1024)S(1)} %get-tuple-element.78, f32[768]{0:T(1024)S(1)} %get-tuple-element.79, f32[128]{0:T(128)S(1)} %add_rsqrt_fusion, ...), kind=kOutput, calls=%fused_computation.8 | convolution fusion | flops 453869568 | bytes 4931584 | tf_op jit(solution)/shard_map/dot_general | solution.py:116
  111.3 1.0 copy-done.9
  112.5 1.2 fusion.87
  117.9 2.3 fusion.23
  120.3 4.7 %fusion.90 = (bf16[3072]{0:T(1024)(128)(2,1)}, bf16[128,3072]{1,0:T(8,128)(2,1)S(1)}) fusion(f32[128,3072]{1,0:T(8,128)S(1)} %fusion.6, bf16[3072,768]{1,0:T(8,128)(2,1)} %bitcast.71, bf16[128,768]{1,0:T(8,128)(2,1)S(1)} %copy-done.3), kind=kOutput, calls=%fused_computation.154 | convolution fusion | flops 608302080 | bytes 7280640 | tf_op jit(solution)/shard_map/dot_general | solution.py:191
  124.9 5.1 %fusion.1 = f32[128,768]{1,0:T(8,128)} fusion(bf16[768,6272]{1,0:T(8,128)(2,1)} %bitcast.101, bf16[128,3072]{1,0:T(8,128)(2,1)S(1)} %get-tuple-element.90), kind=kOutput, calls=%fused_computation.4 | convolution fusion | flops 603979776 | bytes 5898240 | tf_op jit(solution)/shard_map/dot_general | solution.py:195
  130.0 1.7 convolution_convert_fusion.4
  132.1 1.2 fusion.91
  133.3 2.7 %convolution_bitcast_fusion.2 = f32[128,12,64]{0,2,1:T(8,128)} fusion(f32[12,128,128]{1,2,0:T(8,128)} %fusion.91, f32[12,128,128]{1,2,0:T(8,128)S(1)} %get-tuple-element.87, f32[12,128]{1,0:T(8,128)S(1)} %log_add_fusion, bf16[128,12,48]{0,2,1:T(8,128)(2,1)} %copy-done.20, bf16[128,12,8]{0,2,1:T(8,128)(2,1)} %copy-done.34, bf16[128,12,8]{0,2,1:T(8,128)(2,1)} %copy-done.35), kind=kOutput, calls=%fused_computation.30 | convolution fusion | flops 27133568 | bytes 2168832 | tf_op jit(solution)/shard_map/hqk,khd->qhd/dot_general | solution.py:212
  136.0 1.7 slice.175
  137.7 2.6 convolution_bitcast_fusion.1
  141.3 1.0 slice.178
  142.3 1.0 pad_maximum_fusion.1
  143.4 3.5 %fusion.56 = (bf16[768]{0:T(1024)(128)(2,1)S(1)}, f32[128]{0:T(128)S(1)}, f32[128]{0:T(128)S(1)}, bf16[768]{0:T(1024)(128)(2,1)S(1)}, bf16[768]{0:T(1024)(128)(2...) fusion(bf16[128,768]{1,0:T(8,128)(2,1)S(1)} %copy-done, ...), kind=kOutput, calls=%fused_computation.74 | convolution fusion | flops 456421888 | bytes 5716992 | tf_op jit(solution)/shard_map/dot_general | solution.py:229
  147.9 3.0 %convolution_convert_fusion.2 = bf16[768,2304]{1,0:T(8,128)(2,1)} fusion(f32[128,768]{0,1:T(8,128)S(1)} %bitcast.74, f32[128,768]{0,1:T(8,128)S(1)} %bitcast.80, f32[128,768]{0,1:T(8,128)S(1)} %bitcast.77, bf16[128,768]{1,0:T(8,128)(2,1)S(1)} %copy-done, f32[768]{0:T(1024)S(1)} %copy-done.38, f32[768]{0:T(1024)S(1)} %copy-done.30, f32[128]{0:T(128)S(1)} %copy-done.43, ...), kind=kOutput, calls=%fused_computation.3 | convolution fusion | flops 457113600 | bytes 4922368 | tf_op jit(solution)/shard_map/dot_general | solution.py:228
  150.9 1.7 convolution_convert_fusion.3.refs_1_
  152.6 3.6 %convolution_convert_fusion.1 = bf16[768,3072]{1,0:T(8,128)(2,1)} fusion(bf16[128,3072]{1,0:T(8,128)(2,1)S(1)} %copy-done.11, bf16[128,768]{1,0:T(8,128)(2,1)S(1)} %copy-done, f32[768]{0:T(1024)S(1)} %get-tuple-element.76, f32[768]{0:T(1024)S(1)} %get-tuple-element.77, f32[128]{0:T(128)S(1)} %copy-done.43, f32[128]{0:T(128)S(1)} %copy-done.40), kind=kOutput, calls=%fused_computation.2 | convolution fusion | flops 606928896 | bytes 5708800 | tf_op jit(solution)/shard_map/dot_general | solution.py:194
  157.9 3.6 %convolution_convert_fusion = bf16[3072,768]{1,0:T(8,128)(2,1)} fusion(bf16[128,768]{1,0:T(8,128)(2,1)S(1)} %copy-done.3, f32[128,3072]{1,0:T(8,128)S(1)} %fusion.6), kind=kOutput, calls=%fused_computation.1 | convolution fusion | flops 608305152 | bytes 6488064 | tf_op jit(solution)/shard_map/dot_general | solution.py:190
  161.6 93.1 %shard_map.346 = f32[24,9600]{1,0:T(8,128)} custom-call(bf16[32,24,2304]{2,1,0:T(8,128)(2,1)} %bitcast.70, bf16[32,24,768]{2,1,0:T(8,128)(2,1)} %convolution_convert_fusion.3.refs_1_, bf16[32,24,3072]{2,1,0:T(8,128)(2,1)} %bitcast.69, bf16[32,24,384]{2,1,0:T(8,128)(2,1)} %pad.16.refs_3_, bf16[32,96,768]{2,1,0:T(8,128)(2,1)} %bitcast.68), custom_call_target="tpu_custom_call" | custom-call | tf_op jit(solution)/shard_map/pallas_call | solution.py:503
  254.8 2.1 multiply_subtract_fusion.2
  257.7 1.2 slice_multiply_fusion
  260.3 1.0 multiply_subtract_fusion
  (160 shorter events, 18.8 us)
Async XLA Ops:
  0.7 4.3 %copy-start.5 = (f32[96,768]{1,0:T(8,128)S(1)}, f32[96,768]{1,0:T(8,128)}, u32[]{:S(2)}) copy-start(f32[96,768]{1,0:T(8,128)} %param.24) | copy-start | bytes 884740
  2.4 101.0 %copy-start = (bf16[128,768]{1,0:T(8,128)(2,1)S(1)}, bf16[128,768]{1,0:T(8,128)(2,1)}, u32[]{:S(2)}) copy-start(bf16[128,768]{1,0:T(8,128)(2,1)} %param.18) | copy-start | bytes 589828
  103.4 5.1 %copy-start.29 = (f32[768]{0:T(1024)}, f32[768]{0:T(1024)S(1)}, u32[]{:S(2)}) copy-start(f32[768]{0:T(1024)S(1)} %get-tuple-element.79) | copy-start | bytes 9220
  103.4 5.1 %copy-start.37 = (f32[768]{0:T(1024)}, f32[768]{0:T(1024)S(1)}, u32[]{:S(2)}) copy-start(f32[768]{0:T(1024)S(1)} %get-tuple-element.78) | copy-start | bytes 9220
  103.5 5.0 %copy-start.39 = (f32[128]{0:T(128)}, f32[128]{0:T(128)S(1)}, u32[]{:S(2)}) copy-start(f32[128]{0:T(128)S(1)} %broadcast_multiply_fusion.4) | copy-start | bytes 1540
  103.7 4.8 %copy-start.42 = (f32[128]{0:T(128)}, f32[128]{0:T(128)S(1)}, u32[]{:S(2)}) copy-start(f32[128]{0:T(128)S(1)} %add_rsqrt_fusion) | copy-start | bytes 1540
  103.7 3.8 %copy-start.1 = (bf16[32,96,768]{2,1,0:T(8,128)(2,1)S(1)}, bf16[32,96,768]{2,1,0:T(8,128)(2,1)}, u32[]{:S(2)}) copy-start(bf16[32,96,768]{2,1,0:T(8,128)(2,1)} %get-tuple-element.25) | copy-start | bytes 14155780
  112.5 3.3 %copy-start.45 = (s32[1,128]{1,0:T(1,128)S(1)}, s32[1,128]{1,0:T(1,128)}, u32[]{:S(2)}) copy-start(s32[1,128]{1,0:T(1,128)} %param.20) | copy-start | bytes 1540
  124.9 5.1 %copy-start.10 = (bf16[128,3072]{1,0:T(8,128)(2,1)}, bf16[128,3072]{1,0:T(8,128)(2,1)S(1)}, u32[]{:S(2)}) copy-start(bf16[128,3072]{1,0:T(8,128)(2,1)S(1)} %get-tuple-element.90) | copy-start | bytes 2359300
  133.3 4.4 %copy-start.22 = (bf16[128,12,48]{0,2,1:T(8,128)(2,1)S(1)}, bf16[128,12,48]{0,2,1:T(8,128)(2,1)}, u32[]{:S(2)}) copy-start(bf16[128,12,48]{0,2,1:T(8,128)(2,1)} %copy-done.21) | copy-start | bytes 442372
  133.3 4.4 %copy-start.32 = (bf16[128,12,8]{0,2,1:T(8,128)(2,1)S(1)}, bf16[128,12,8]{0,2,1:T(8,128)(2,1)}, u32[]{:S(2)}) copy-start(bf16[128,12,8]{0,2,1:T(8,128)(2,1)} %copy-done.31) | copy-start | bytes 73732
  136.0 4.3 %copy-start.26 = (f32[128,8]{0,1:T(8,128)S(1)}, f32[128,8]{0,1:T(8,128)}, u32[]{:S(2)}) copy-start(f32[128,8]{0,1:T(8,128)} %copy-done.25) | copy-start | bytes 12292
  136.0 4.3 %copy-start.28 = (f32[128,8]{0,1:T(8,128)S(1)}, f32[128,8]{0,1:T(8,128)}, u32[]{:S(2)}) copy-start(f32[128,8]{0,1:T(8,128)} %copy-done.27) | copy-start | bytes 12292
  140.3 3.0 %copy-start.30 = (f32[768]{0:T(1024)S(1)}, f32[768]{0:T(1024)}, u32[]{:S(2)}) copy-start(f32[768]{0:T(1024)} %copy-done.29) | copy-start | bytes 9220
  140.3 3.0 %copy-start.40 = (f32[128]{0:T(128)S(1)}, f32[128]{0:T(128)}, u32[]{:S(2)}) copy-start(f32[128]{0:T(128)} %copy-done.39) | copy-start | bytes 1540
  140.3 3.0 %copy-start.43 = (f32[128]{0:T(128)S(1)}, f32[128]{0:T(128)}, u32[]{:S(2)}) copy-start(f32[128]{0:T(128)} %copy-done.42) | copy-start | bytes 1540
  143.4 4.5 %copy-start.38 = (f32[768]{0:T(1024)S(1)}, f32[768]{0:T(1024)}, u32[]{:S(2)}) copy-start(f32[768]{0:T(1024)} %copy-done.37) | copy-start | bytes 9220
  152.6 4.2 %copy-start.44 = (bf16[3072]{0:T(1024)(128)(2,1)S(1)}, bf16[3072]{0:T(1024)(128)(2,1)}, u32[]{:S(2)}) copy-start(bf16[3072]{0:T(1024)(128)(2,1)} %get-tuple-element.89) | copy-start | bytes 18436
  161.6 93.2 %copy-start.8 = (f32[24,2304]{1,0:T(8,128)S(1)}, f32[24,2304]{1,0:T(8,128)}, u32[]{:S(2)}) copy-start(f32[24,2304]{1,0:T(8,128)} %param.21) | copy-start | bytes 663556
  161.6 93.2 %copy-start.18 = (f32[24,2304]{1,0:T(8,128)S(1)}, f32[24,2304]{1,0:T(8,128)}, u32[]{:S(2)}) copy-start(f32[24,2304]{1,0:T(8,128)} %param.26) | copy-start | bytes 663556
  161.6 93.2 %copy-start.19 = (f32[24,2304]{1,0:T(8,128)S(1)}, f32[24,2304]{1,0:T(8,128)}, u32[]{:S(2)}) copy-start(f32[24,2304]{1,0:T(8,128)} %param.31) | copy-start | bytes 663556
  161.6 95.3 %copy-start.15 = (f32[24,768]{1,0:T(8,128)S(1)}, f32[24,768]{1,0:T(8,128)}, u32[]{:S(2)}) copy-start(f32[24,768]{1,0:T(8,128)} %param.22) | copy-start | bytes 221188
  161.6 95.3 %copy-start.23 = (f32[24,768]{1,0:T(8,128)S(1)}, f32[24,768]{1,0:T(8,128)}, u32[]{:S(2)}) copy-start(f32[24,768]{1,0:T(8,128)} %param.27) | copy-start | bytes 221188
  161.6 95.3 %copy-start.24 = (f32[24,768]{1,0:T(8,128)S(1)}, f32[24,768]{1,0:T(8,128)}, u32[]{:S(2)}) copy-start(f32[24,768]{1,0:T(8,128)} %param.32) | copy-start | bytes 221188
  (24 other events, 39.3 us)

commit v2 on v1

--- a/solution.py
+++ b/solution.py
@@ -245,6 +245,7 @@
         + layer_norm_back(grad_hidden_one, normed_one, sigma_one, vec_table[0])
         + layer_norm_back(grad_hidden_two, normed_two, sigma_two, vec_table[2])
     ).astype(jnp.bfloat16)
+    grad_table = lax.optimization_barrier(grad_table)
     return (grad_tokens, grad_w_qkv, grad_w_out, grad_w_up, grad_w_down, grad_table.reshape(-1))
 
 
@@ -263,6 +264,7 @@
 LANES = 128
 VEC_WIDE = 3 * LANES
 STEP_WIDE = 5 * LANES
+CHUNKS = 5
 
 
 class Place:
@@ -300,7 +302,7 @@
 
 
 def gather_kernel(side, fsdp, *refs):
-    kinds = 2
+    kinds = 3
     shards, wholes = refs[:kinds], refs[kinds : 2 * kinds]
     wired, paired, sent, kept = refs[2 * kinds :]
     here = Place(side, fsdp)
@@ -312,63 +314,64 @@
     ]
     here.greet()
 
-    def push(origin, hop):
+    def push(origin, hop, i):
         first, second, level = origin
         slot = here.rank(first, second, level)
+        source = shards[i] if origin == (0, 0, 0) else wholes[i].at[slot]
+        if hop is None:
+            peer = here.device(0, 0, 0, None, 1 - here.core)
+            arrival = paired.at[here.number(first, second, level), i]
+        else:
+            peer = here.device(*hop)
+            arrival = wired.at[
+                here.number(
+                    (first - hop[0]) % side, (second - hop[1]) % side, (level - hop[2]) % depth
+                ),
+                i,
+            ]
+        pltpu.make_async_remote_copy(
+            src_ref=source,
+            dst_ref=wholes[i].at[slot],
+            send_sem=sent.at[i],
+            recv_sem=arrival,
+            device_id=peer,
+            device_id_type=MESH,
+        ).start()
+
+    def arrive(origin, sems, owner, i):
+        slot = here.rank(*origin, owner)
+        pltpu.make_async_copy(
+            wholes[i].at[slot], wholes[i].at[slot], sems.at[here.number(*origin), i]
+        ).wait()
+
+    def relay(origin, hops):
         for i in range(kinds):
-            source = shards[i] if origin == (0, 0, 0) else wholes[i].at[slot]
-            if hop is None:
-                peer = here.device(0, 0, 0, None, 1 - here.core)
-                arrival = paired.at[here.number(first, second, level), i]
-            else:
-                peer = here.device(*hop)
-                arrival = wired.at[
-                    here.number(
-                        (first - hop[0]) % side, (second - hop[1]) % side, (level - hop[2]) % depth
-                    ),
-                    i,
-                ]
-            pltpu.make_async_remote_copy(
-                src_ref=source,
-                dst_ref=wholes[i].at[slot],
-                send_sem=sent.at[i],
-                recv_sem=arrival,
-                device_id=peer,
-                device_id_type=MESH,
-            ).start()
-
-    def arrive(origin, sems, owner):
-        slot = here.rank(*origin, owner)
-        for i in range(kinds):
-            pltpu.make_async_copy(
-                wholes[i].at[slot], wholes[i].at[slot], sems.at[here.number(*origin), i]
-            ).wait()
+            arrive(origin, wired, here.core, i)
+            for hop in hops:
+                push(origin, hop, i)
 
     first_hops = [(k, 0, 0) for k in range(1, side)]
     second_hops = [(0, k, 0) for k in range(1, side)]
     level_hops = [(0, 0, k) for k in range(1, depth)]
-    for hop in second_hops + first_hops + level_hops + [None]:
-        push((0, 0, 0), hop)
+    for i in range(kinds):
+        for hop in level_hops + second_hops + first_hops + [None]:
+            push((0, 0, 0), hop, i)
     for copy in local:
         copy.start()
-    for level in range(1, depth):
-        arrive((0, 0, level), wired, here.core)
-        for hop in second_hops + first_hops + [None]:
-            push((0, 0, level), hop)
+    for level in range(1, depth + 1):
+        if level < depth:
+            relay((0, 0, level), second_hops + first_hops + [None])
+        for first in range(1, side):
+            relay((first, 0, level - 1), second_hops + [None])
     for level in range(depth):
-        for first in range(1, side):
-            arrive((first, 0, level), wired, here.core)
-            for hop in second_hops + [None]:
-                push((first, 0, level), hop)
-    for first in range(side):
-        for level in range(depth):
+        for first in range(side):
             for second in range(1, side):
-                arrive((first, second, level), wired, here.core)
-                push((first, second, level), None)
-    for second in range(side):
-        for first in range(side):
-            for level in range(depth):
-                arrive((first, second, level), paired, 1 - here.core)
+                relay((first, second, level), [None])
+    for level in range(depth):
+        for second in range(side):
+            for first in range(side):
+                for i in range(kinds):
+                    arrive((first, second, level), paired, 1 - here.core, i)
     for copy in local:
         copy.wait()
     for i in range(kinds):
@@ -403,41 +406,46 @@
     wide = total.shape[1]
     here.greet()
 
-    pieces, at = [], 0
+    span = wide // CHUNKS
+    pieces, at = [[] for _ in range(CHUNKS)], 0
     for part in parts:
         for block in range(part.shape[1] // rows):
-            pieces.append((part, block * rows, at, part.shape[2]))
-            at += part.shape[2]
+            start, end = at, at + part.shape[2]
+            while at < end:
+                chunk, width = at // span, min(end, (at // span + 1) * span) - at
+                pieces[chunk].append((part, block * rows, at - start, at - chunk * span, width))
+                at += width
 
     firsts = list(range(1, side)) + [0]
     levels = list(range(1, depth)) + [0]
     order = [(f, s, k) for s in firsts for f in firsts for k in levels]
-    for first, second, level in order:
-        index = here.number(first, second, level)
-        theirs = here.rank(first, second, level, 1 - here.core)
-        ours = here.rank(first, second, level)
-        for part, row, column, width in pieces:
-            pltpu.make_async_remote_copy(
-                src_ref=part.at[theirs, pl.ds(row, rows)],
-                dst_ref=pair.at[index, :, pl.ds(column, width)],
-                send_sem=sent_pair,
-                recv_sem=pair_sem.at[index],
-                device_id=here.device(0, 0, 0, None, 1 - here.core),
-                device_id_type=MESH,
-            ).start()
-        for part, row, column, width in pieces:
-            pltpu.make_async_copy(
-                part.at[ours, pl.ds(row, rows)],
-                mine.at[index, :, pl.ds(column, width)],
-                load_sem.at[index],
-            ).start()
-
-    def send(index, target, slot, number, hop):
+    for chunk in range(CHUNKS):
+        for first, second, level in order:
+            index = here.number(first, second, level)
+            theirs = here.rank(first, second, level, 1 - here.core)
+            ours = here.rank(first, second, level)
+            for part, row, source, column, width in pieces[chunk]:
+                pltpu.make_async_remote_copy(
+                    src_ref=part.at[theirs, pl.ds(row, rows), pl.ds(source, width)],
+                    dst_ref=pair.at[chunk, index, :, pl.ds(column, width)],
+                    send_sem=sent_pair,
+                    recv_sem=pair_sem.at[chunk, index],
+                    device_id=here.device(0, 0, 0, None, 1 - here.core),
+                    device_id_type=MESH,
+                ).start()
+            for part, row, source, column, width in pieces[chunk]:
+                pltpu.make_async_copy(
+                    part.at[ours, pl.ds(row, rows), pl.ds(source, width)],
+                    mine.at[chunk, index, :, pl.ds(column, width)],
+                    load_sem.at[chunk, index],
+                ).start()
+
+    def send(chunk, index, target, slot, number, hop):
         pltpu.make_async_remote_copy(
-            src_ref=mine.at[index],
-            dst_ref=target.at[slot],
-            send_sem=sent.at[index],
-            recv_sem=wire_sem.at[number],
+            src_ref=mine.at[chunk, index],
+            dst_ref=target.at[chunk, slot],
+            send_sem=sent.at[chunk, index],
+            recv_sem=wire_sem.at[chunk, number],
             device_id=here.device(*hop),
             device_id_type=MESH,
         ).start()
@@ -449,50 +457,64 @@
     first_slot = lambda first, level: (first - 1) * depth + level
     base_two = (side - 1) * side * depth
     base_three = base_two + (side - 1) * depth
-    for first, second, level in order:
+
+    def handle(chunk, first, second, level):
         index = here.number(first, second, level)
-        landed(mine.at[index], load_sem.at[index])
-        landed(pair.at[index], pair_sem.at[index])
-        terms = [mine.at[index], pair.at[index]]
+        landed(mine.at[chunk, index], load_sem.at[chunk, index])
+        landed(pair.at[chunk, index], pair_sem.at[chunk, index])
+        terms = [mine.at[chunk, index], pair.at[chunk, index]]
         if second == 0:
             for k in range(1, side):
                 slot = second_slot(k, first, level)
-                landed(one.at[slot], wire_sem.at[slot])
-                terms.append(one.at[slot])
+                landed(one.at[chunk, slot], wire_sem.at[chunk, slot])
+                terms.append(one.at[chunk, slot])
             if first == 0:
                 for k in range(1, side):
                     slot = first_slot(k, level)
-                    landed(two.at[slot], wire_sem.at[base_two + slot])
-                    terms.append(two.at[slot])
+                    landed(two.at[chunk, slot], wire_sem.at[chunk, base_two + slot])
+                    terms.append(two.at[chunk, slot])
                 if level == 0:
                     for k in range(1, depth):
-                        landed(three.at[k - 1], wire_sem.at[base_three + k - 1])
-                        terms.append(three.at[k - 1])
+                        landed(three.at[chunk, k - 1], wire_sem.at[chunk, base_three + k - 1])
+                        terms.append(three.at[chunk, k - 1])
         last = (first, second, level) == (0, 0, 0)
 
-        @pl.loop(0, wide // STEP_WIDE)
+        @pl.loop(0, span // STEP_WIDE)
         def _(step):
             columns = pl.ds(pl.multiple_of(step * STEP_WIDE, LANES), STEP_WIDE)
             value = terms[0][:, columns].astype(jnp.float32)
             for term in terms[1:]:
                 value = value + term[:, columns].astype(jnp.float32)
             if last:
-                total[:, columns] = value
+                place = pl.ds(pl.multiple_of(chunk * span + step * STEP_WIDE, LANES), STEP_WIDE)
+                total[:, place] = value
             else:
-                mine[index, :, columns] = value.astype(jnp.bfloat16)
+                mine[chunk, index, :, columns] = value.astype(jnp.bfloat16)
 
         if second:
             slot = second_slot(second, first, level)
-            send(index, one, slot, slot, (0, second, 0))
+            send(chunk, index, one, slot, slot, (0, second, 0))
         elif first:
             slot = first_slot(first, level)
-            send(index, two, slot, base_two + slot, (first, 0, 0))
+            send(chunk, index, two, slot, base_two + slot, (first, 0, 0))
         elif level:
-            send(index, three, level - 1, base_three + level - 1, (0, 0, level))
+            send(chunk, index, three, level - 1, base_three + level - 1, (0, 0, level))
+
+    stages = [[], [], [], []]
+    for first, second, level in order:
+        stage = 0 if second else 1 if first else 2 if level else 3
+        stages[stage].append((first, second, level))
+    for tick in range(CHUNKS + len(stages) + 2):
+        for stage in range(len(stages)):
+            chunk = tick - stage
+            if 0 <= chunk < CHUNKS:
+                for item in stages[stage]:
+                    handle(chunk, *item)
     landed(pair, sent_pair)
-    for first, second, level in order[:-1]:
-        index = here.number(first, second, level)
-        landed(mine.at[index], sent.at[index])
+    for chunk in range(CHUNKS):
+        for first, second, level in order[:-1]:
+            index = here.number(first, second, level)
+            landed(mine.at[chunk, index], sent.at[chunk, index])
 
 
 def scatter_sums(parts, side, fsdp):
@@ -506,14 +528,15 @@
         in_specs=[pl.BlockSpec(memory_space=pl.ANY)] * 5,
         out_specs=pl.BlockSpec(memory_space=pltpu.VMEM),
         scratch_shapes=[
-            pltpu.VMEM((n, rows, wide), jnp.bfloat16) for n in [half, half, *stages]
+            pltpu.VMEM((CHUNKS, n, rows, wide // CHUNKS), jnp.bfloat16)
+            for n in [half, half, *stages]
         ]
         + [
-            pltpu.SemaphoreType.DMA((half,)),
-            pltpu.SemaphoreType.DMA((half,)),
-            pltpu.SemaphoreType.DMA((sum(stages),)),
+            pltpu.SemaphoreType.DMA((CHUNKS, half)),
+            pltpu.SemaphoreType.DMA((CHUNKS, half)),
+            pltpu.SemaphoreType.DMA((CHUNKS, sum(stages))),
             pltpu.SemaphoreType.DMA,
-            pltpu.SemaphoreType.DMA((half,)),
+            pltpu.SemaphoreType.DMA((CHUNKS, half)),
         ],
         compiler_params=pltpu.CompilerParams(
             collective_id=1, has_side_effects=True, vmem_limit_bytes=56 << 20
@@ -525,17 +548,16 @@
     rows, count = w_qkv.shape[0], side * side * fsdp
     low = [x.astype(jnp.bfloat16) for x in (w_qkv, w_out, w_up, w_down, vectors)]
     vec = jnp.pad(low[4], (0, rows * LANES - vectors.shape[0])).reshape(rows, LANES)
-    packed, full_down = gather_shards(
-        (jnp.concatenate([low[0], low[1], low[2], vec], axis=1), low[3]), side, fsdp
+    packed, full_up, full_down = gather_shards(
+        (jnp.concatenate([low[0], low[1], vec], axis=1), low[2], low[3]), side, fsdp
     )
     packed = packed.reshape(count * rows, -1)
-    ends = [w_qkv.shape[1], w_out.shape[1], w_up.shape[1]]
-    one, two, three = ends[0], ends[0] + ends[1], sum(ends)
-    full_vec = packed[:, three:].reshape(count, rows * LANES)[:, : vectors.shape[0]].reshape(-1)
+    one, two = w_qkv.shape[1], w_qkv.shape[1] + w_out.shape[1]
+    full_vec = packed[:, two:].reshape(count, rows * LANES)[:, : vectors.shape[0]].reshape(-1)
     return (
         packed[:, :one],
         packed[:, one:two],
-        packed[:, two:three],
+        full_up.reshape(-1, w_up.shape[1]),
         full_down.reshape(-1, w_down.shape[1]),
         full_vec,
     )

time: 262 us -> 242 us (0.924)
  Pallas kernels: 189 us -> 168 us
    pallas_call x1, Pallas kernels: 93.1 us -> 78.7 us  [scatter_sums(): pl.pallas_call(functools.partial(scatter_kernel, side, fsdp), out_shape=j...]
    pallas_call x1, Pallas kernels: 95.9 us -> 89.4 us  [gather_shards(): pl.pallas_call(functools.partial(gather_kernel, side, fsdp), out_shape=[j...]
    dot_general x1, matrix products: 5.09 us -> 2.44 us  [backward_pass(): jnp.dot(grad_up_low, back_up.T, preferred_element_type=jnp.float32)]
where the time goes in v2:
time: 242 us; the launch traced here: 239 us
  Pallas kernels  168 us (69%)
  matrix products  41.2 us (17%)
  other arithmetic  17.2 us (7%)
  local copies, waits for them, and re-layouts  11.4 us (5%)
    pallas_call x1, Pallas kernels, gather_shards(): pl.pallas_call(functools.partial(gather_kernel, side, fsdp), out_shape=[j...  89.4 us
    pallas_call x1, Pallas kernels, scatter_sums(): pl.pallas_call(functools.partial(scatter_kernel, side, fsdp), out_shape=j...  78.7 us
    convert_element_type x5, other arithmetic, gather_all(): x.astype(jnp.bfloat16)  5.84 us

profile of v2, /device:TPU:9, one launch (start us, length us, event | category | flops | bytes accessed | tf_op | source)
XLA Modules:
  0.0 239.4 jit_solution(2413953564458196639)
XLA Ops:
  3.9 1.6 convert_element_type.116.refs_1_
  5.6 1.6 convert_element_type.117.refs_2_
  7.2 89.4 %shard_map.345 = (bf16[32,24,3200]{2,1,0:T(8,128)(2,1)}, bf16[32,24,3072]{2,1,0:T(8,128)(2,1)}, bf16[32,96,768]{2,1,0:T(8,128)(2,1)}) custom-call(bf16[24,3200]{1,0:T(8,128)(2,1)} %pad_maximum_fusion.5.refs_0_, bf16[24,3072]{1,0:T(8,128)(2,1)} %convert_element_type.116.refs_1_, bf16[96,768]{1,0:T(8,128)(2,1)} %convert_element_type.117.refs_2_), custom_call_target="tpu_custom_call" | custom-call | tf_op jit(solution)/shard_map/pallas_call | solution.py:385
  98.8 3.3 %convolution_add_fusion.1 = f32[128,3072]{1,0:T(8,128)S(1)} fusion(bf16[768,3072]{1,0:T(8,128)(2,1)} %bitcast.73, f32[3072]{0:T(1024)S(1)} %slice.166, bf16[128,768]{1,0:T(8,128)(2,1)S(1)} %copy-done, f32[768]{0:T(1024)S(1)} %get-tuple-element.80, f32[768]{0:T(1024)S(1)} %get-tuple-element.81, f32[128]{0:T(128)S(1)} %add_rsqrt_fusion, ...), kind=kOutput, calls=%fused_computation.7 | convolution fusion | flops 604962816 | bytes 6507520 | tf_op jit(solution)/shard_map/dot_general | solution.py:136
  103.5 2.7 %convolution_add_fusion = f32[128,2304]{1,0:T(8,128)S(1)} fusion(bf16[768,3200]{1,0:T(8,128)(2,1)} %bitcast.105, f32[2304]{0:T(1024)S(1)} %slice.152, bf16[128,768]{1,0:T(8,128)(2,1)S(1)} %copy-done, f32[768]{0:T(1024)S(1)} %get-tuple-element.82, f32[768]{0:T(1024)S(1)} %get-tuple-element.83, f32[128]{0:T(128)S(1)} %add_rsqrt_fusion, ...), kind=kOutput, calls=%fused_computation.4 | convolution fusion | flops 453869568 | bytes 4931584 | tf_op jit(solution)/shard_map/dot_general | solution.py:116
  107.4 1.2 fusion.80
  112.9 2.5 %fusion.16 = bf16[128,768]{1,0:T(8,128)(2,1)} fusion(f32[128,768]{1,0:T(8,128)S(1)} %convolution_add_fusion.3, bf16[128,768]{0,1:T(8,128)(2,1)S(1)} %bitcast.89, bf16[768,3200]{1,0:T(8,128)(2,1)} %bitcast.106, bf16[128,768]{1,0:T(8,128)(2,1)S(1)} %copy-done, f32[768]{0:T(1024)S(1)} %copy-done.36), kind=kOutput, calls=%fused_computation.32 | convolution fusion | flops 151486464 | bytes 2165760 | tf_op jit(solution)/shard_map/dot_general | solution.py:135
  115.4 4.7 %fusion.83 = (bf16[3072]{0:T(1024)(128)(2,1)}, bf16[128,3072]{1,0:T(8,128)(2,1)S(1)}) fusion(f32[128,3072]{1,0:T(8,128)S(1)} %convolution_add_fusion.1, bf16[3072,768]{1,0:T(8,128)(2,1)} %bitcast.78, bf16[128,768]{1,0:T(8,128)(2,1)S(1)} %copy-done.5), kind=kOutput, calls=%fused_computation.152 | convolution fusion | flops 608302080 | bytes 7280640 | tf_op jit(solution)/shard_map/dot_general | solution.py:191
  120.1 2.4 %fusion.52 = f32[128,768]{1,0:T(8,128)} fusion(bf16[768,3072]{1,0:T(8,128)(2,1)S(1)} %bitcast.76, bf16[128,3072]{1,0:T(8,128)(2,1)S(1)} %get-tuple-element.94), kind=kOutput, calls=%fused_computation.78 | convolution fusion | flops 603979776 | bytes 5898240 | tf_op jit(solution)/shard_map/dot_general | solution.py:195
  122.6 1.7 convolution_convert_fusion.4
  124.7 1.2 fusion.84
  125.9 2.7 %convolution_bitcast_fusion.2 = f32[128,12,64]{0,2,1:T(8,128)} fusion(f32[12,128,128]{1,2,0:T(8,128)} %fusion.84, f32[12,128,128]{1,2,0:T(8,128)S(1)} %get-tuple-element.91, f32[12,128]{1,0:T(8,128)S(1)} %log_add_fusion, bf16[128,12,48]{0,2,1:T(8,128)(2,1)} %copy-done.19, bf16[128,12,8]{0,2,1:T(8,128)(2,1)} %copy-done.32, bf16[128,12,8]{0,2,1:T(8,128)(2,1)} %copy-done.33), kind=kOutput, calls=%fused_computation.26 | convolution fusion | flops 27133568 | bytes 2168832 | tf_op jit(solution)/shard_map/hqk,khd->qhd/dot_general | solution.py:212
  128.6 1.7 slice.170
  130.3 2.5 %convolution_bitcast_fusion.1 = f32[128,12,64]{0,2,1:T(8,128)} fusion(f32[12,128,128]{1,2,0:T(8,128)} %fusion.84, f32[12,128,128]{1,2,0:T(8,128)S(1)} %get-tuple-element.91, f32[12,128]{1,0:T(8,128)S(1)} %log_add_fusion, bf16[128,12,48]{0,2,1:T(8,128)(2,1)S(1)} %copy-done.21, bf16[128,12,8]{0,2,1:T(8,128)(2,1)S(1)} %copy-done.31, ...), kind=kOutput, calls=%fused_computation.25 | convolution fusion | flops 27133568 | bytes 2168832 | tf_op jit(solution)/shard_map/hqk,qhd->khd/dot_general | solution.py:215
  134.8 1.0 pad_maximum_fusion.1
  135.9 3.5 %fusion.48 = (bf16[768]{0:T(1024)(128)(2,1)S(1)}, f32[128]{0:T(128)S(1)}, f32[128]{0:T(128)S(1)}, bf16[768]{0:T(1024)(128)(2,1)S(1)}, bf16[768]{0:T(1024)(128)(2...) fusion(bf16[128,768]{1,0:T(8,128)(2,1)S(1)} %copy-done, ...), kind=kOutput, calls=%fused_computation.71 | convolution fusion | flops 456421888 | bytes 5716992 | tf_op jit(solution)/shard_map/dot_general | solution.py:229
  140.5 3.2 %convolution_convert_fusion.2 = bf16[768,2304]{1,0:T(8,128)(2,1)} fusion(f32[128,768]{0,1:T(8,128)S(1)} %bitcast.81, f32[128,768]{0,1:T(8,128)S(1)} %bitcast.87, f32[128,768]{0,1:T(8,128)S(1)} %bitcast.84, bf16[128,768]{1,0:T(8,128)(2,1)S(1)} %copy-done, f32[768]{0:T(1024)S(1)} %copy-done.38, f32[768]{0:T(1024)S(1)} %copy-done.27, f32[128]{0:T(128)S(1)} %copy-done.40, ...), kind=kOutput, calls=%fused_computation.3 | convolution fusion | flops 457113600 | bytes 4922368 | tf_op jit(solution)/shard_map/dot_general | solution.py:228
  143.7 1.5 convolution_convert_fusion.3.refs_1_
  145.2 3.6 %convolution_convert_fusion.1 = bf16[768,3072]{1,0:T(8,128)(2,1)} fusion(bf16[128,3072]{1,0:T(8,128)(2,1)S(1)} %copy-done.4, bf16[128,768]{1,0:T(8,128)(2,1)S(1)} %copy-done, f32[768]{0:T(1024)S(1)} %get-tuple-element.80, f32[768]{0:T(1024)S(1)} %get-tuple-element.81, f32[128]{0:T(128)S(1)} %copy-done.40, f32[128]{0:T(128)S(1)} %copy-done.35), kind=kOutput, calls=%fused_computation.2 | convolution fusion | flops 606928896 | bytes 5708800 | tf_op jit(solution)/shard_map/dot_general | solution.py:194
  150.4 3.6 %convolution_convert_fusion = bf16[3072,768]{1,0:T(8,128)(2,1)} fusion(bf16[128,768]{1,0:T(8,128)(2,1)S(1)} %copy-done.5, f32[128,3072]{1,0:T(8,128)S(1)} %convolution_add_fusion.1), kind=kOutput, calls=%fused_computation.1 | convolution fusion | flops 608305152 | bytes 6488064 | tf_op jit(solution)/shard_map/dot_general | solution.py:190
  154.1 78.7 %shard_map.346 = f32[24,9600]{1,0:T(8,128)} custom-call(bf16[32,24,2304]{2,1,0:T(8,128)(2,1)} %bitcast.77, bf16[32,24,768]{2,1,0:T(8,128)(2,1)} %convolution_convert_fusion.3.refs_1_, bf16[32,24,3072]{2,1,0:T(8,128)(2,1)} %bitcast.72, bf16[32,24,384]{2,1,0:T(8,128)(2,1)} %pad.16.refs_3_, bf16[32,96,768]{2,1,0:T(8,128)(2,1)} %bitcast.71), custom_call_target="tpu_custom_call" | custom-call | tf_op jit(solution)/shard_map/pallas_call | solution.py:525
  232.8 2.1 multiply_subtract_fusion.2
  235.7 1.2 slice_multiply_fusion
  238.3 1.0 multiply_subtract_fusion
  (160 shorter events, 19.0 us)
Async XLA Ops:
  0.7 97.7 %copy-start = (bf16[128,768]{1,0:T(8,128)(2,1)S(1)}, bf16[128,768]{1,0:T(8,128)(2,1)}, u32[]{:S(2)}) copy-start(bf16[128,768]{1,0:T(8,128)(2,1)} %param.18) | copy-start | bytes 589828
  98.4 5.1 %copy-start.26 = (f32[768]{0:T(1024)}, f32[768]{0:T(1024)S(1)}, u32[]{:S(2)}) copy-start(f32[768]{0:T(1024)S(1)} %get-tuple-element.83) | copy-start | bytes 9220
  98.4 5.1 %copy-start.37 = (f32[768]{0:T(1024)}, f32[768]{0:T(1024)S(1)}, u32[]{:S(2)}) copy-start(f32[768]{0:T(1024)S(1)} %get-tuple-element.82) | copy-start | bytes 9220
  98.5 5.0 %copy-start.34 = (f32[128]{0:T(128)}, f32[128]{0:T(128)S(1)}, u32[]{:S(2)}) copy-start(f32[128]{0:T(128)S(1)} %broadcast_multiply_fusion.4) | copy-start | bytes 1540
  98.7 4.8 %copy-start.39 = (f32[128]{0:T(128)}, f32[128]{0:T(128)S(1)}, u32[]{:S(2)}) copy-start(f32[128]{0:T(128)S(1)} %add_rsqrt_fusion) | copy-start | bytes 1540
  98.7 3.8 %copy-start.1 = (bf16[32,96,768]{2,1,0:T(8,128)(2,1)S(1)}, bf16[32,96,768]{2,1,0:T(8,128)(2,1)}, u32[]{:S(2)}) copy-start(bf16[32,96,768]{2,1,0:T(8,128)(2,1)} %get-tuple-element.27) | copy-start | bytes 14155780
  107.4 3.3 %copy-start.43 = (s32[1,128]{1,0:T(1,128)S(1)}, s32[1,128]{1,0:T(1,128)}, u32[]{:S(2)}) copy-start(s32[1,128]{1,0:T(1,128)} %param.20) | copy-start | bytes 1540
  112.9 7.2 %slice-start = ((s8[4718592]{0:T(1024)(128)(4,1)}), s8[4194304]{0:T(1024)(128)(4,1)S(1)}, s32[]{:S(2)}) async-start(s8[4718592]{0:T(1024)(128)(4,1)} %bitcast.74), calls=%async_computation | async-start | bytes 8388608
  115.4 4.7 %slice-start.1 = ((s8[4718592]{0:T(1024)(128)(4,1)}), s8[524288]{0:T(1024)(128)(4,1)S(1)}, s32[]{:S(2)}) async-start(s8[4718592]{0:T(1024)(128)(4,1)} %bitcast.74), calls=%async_computation.1 | async-start | bytes 1048576
  125.9 4.4 %copy-start.21 = (bf16[128,12,48]{0,2,1:T(8,128)(2,1)S(1)}, bf16[128,12,48]{0,2,1:T(8,128)(2,1)}, u32[]{:S(2)}) copy-start(bf16[128,12,48]{0,2,1:T(8,128)(2,1)} %copy-done.20) | copy-start | bytes 442372
  125.9 4.4 %copy-start.29 = (bf16[128,12,8]{0,2,1:T(8,128)(2,1)S(1)}, bf16[128,12,8]{0,2,1:T(8,128)(2,1)}, u32[]{:S(2)}) copy-start(bf16[128,12,8]{0,2,1:T(8,128)(2,1)} %copy-done.28) | copy-start | bytes 73732
  125.9 4.4 %copy-start.31 = (bf16[128,12,8]{0,2,1:T(8,128)(2,1)S(1)}, bf16[128,12,8]{0,2,1:T(8,128)(2,1)}, u32[]{:S(2)}) copy-start(bf16[128,12,8]{0,2,1:T(8,128)(2,1)} %copy-done.30) | copy-start | bytes 73732
  132.8 3.0 %copy-start.6 = (f32[128,768]{1,0:T(8,128)S(1)}, f32[128,768]{1,0:T(8,128)}, u32[]{:S(2)}) copy-start(f32[128,768]{1,0:T(8,128)} %fusion.52) | copy-start | bytes 1179652
  132.8 3.0 %copy-start.27 = (f32[768]{0:T(1024)S(1)}, f32[768]{0:T(1024)}, u32[]{:S(2)}) copy-start(f32[768]{0:T(1024)} %copy-done.26) | copy-start | bytes 9220
  132.8 3.1 %copy-start.35 = (f32[128]{0:T(128)S(1)}, f32[128]{0:T(128)}, u32[]{:S(2)}) copy-start(f32[128]{0:T(128)} %copy-done.34) | copy-start | bytes 1540
  132.8 3.1 %copy-start.40 = (f32[128]{0:T(128)S(1)}, f32[128]{0:T(128)}, u32[]{:S(2)}) copy-start(f32[128]{0:T(128)} %copy-done.39) | copy-start | bytes 1540
  135.9 4.6 %copy-start.38 = (f32[768]{0:T(1024)S(1)}, f32[768]{0:T(1024)}, u32[]{:S(2)}) copy-start(f32[768]{0:T(1024)} %copy-done.37) | copy-start | bytes 9220
  145.2 4.1 %copy-start.42 = (bf16[3072]{0:T(1024)(128)(2,1)S(1)}, bf16[3072]{0:T(1024)(128)(2,1)}, u32[]{:S(2)}) copy-start(bf16[3072]{0:T(1024)(128)(2,1)} %get-tuple-element.93) | copy-start | bytes 18436
  154.0 78.7 %copy-start.10 = (f32[24,2304]{1,0:T(8,128)S(1)}, f32[24,2304]{1,0:T(8,128)}, u32[]{:S(2)}) copy-start(f32[24,2304]{1,0:T(8,128)} %param.21) | copy-start | bytes 663556
  154.0 78.7 %copy-start.17 = (f32[24,2304]{1,0:T(8,128)S(1)}, f32[24,2304]{1,0:T(8,128)}, u32[]{:S(2)}) copy-start(f32[24,2304]{1,0:T(8,128)} %param.26) | copy-start | bytes 663556
  154.1 78.7 %copy-start.18 = (f32[24,2304]{1,0:T(8,128)S(1)}, f32[24,2304]{1,0:T(8,128)}, u32[]{:S(2)}) copy-start(f32[24,2304]{1,0:T(8,128)} %param.31) | copy-start | bytes 663556
  154.1 80.9 %copy-start.14 = (f32[24,768]{1,0:T(8,128)S(1)}, f32[24,768]{1,0:T(8,128)}, u32[]{:S(2)}) copy-start(f32[24,768]{1,0:T(8,128)} %param.22) | copy-start | bytes 221188
  154.1 80.9 %copy-start.22 = (f32[24,768]{1,0:T(8,128)S(1)}, f32[24,768]{1,0:T(8,128)}, u32[]{:S(2)}) copy-start(f32[24,768]{1,0:T(8,128)} %param.27) | copy-start | bytes 221188
  154.1 80.9 %copy-start.23 = (f32[24,768]{1,0:T(8,128)S(1)}, f32[24,768]{1,0:T(8,128)}, u32[]{:S(2)}) copy-start(f32[24,768]{1,0:T(8,128)} %param.32) | copy-start | bytes 221188
  (24 other events, 38.7 us)
